TPU v7x, 32 devices: a whole 2x2x4 slice. The times are simulated.
32 devices in a mesh: row: 8 (over z, x), col: 4 (over y, core).
Axes of the slice: x: 2, y: 2, z: 4, core: 2. Of those that a mesh axis runs over, the one named last changes fastest.
Arguments:
- vectors: float32 [8, 4096], P(None, ('row', 'col')), may hold values from -6 to 6
- values: float32 [512, 16384], P('row', 'col'), may hold values from -1 to 1
- block_rows: int32 [8, 256], P('row', 'col'), may hold values from 0 to 7
- block_cols: int32 [8, 256], P('row', 'col'), may hold values from 0 to 15
- counts: int32 [8, 4], P('row', 'col'), may hold values from 16 to 64, as said below
Outputs:
- product: float32 [8, 4096], P(None, ('row', 'col'))
Inputs may be any that keep to these rules, and one draw needn't show every extreme that they name: counts[r, c] slots of tile (r, c) hold blocks, the others are unused; some tile uses all 64 slots.
All inputs are finite; a program needn't handle non-finite values.
Results may differ from a plain program's by a relative error of at most 0.0003.
Values sent between devices are 32-bit elements; how exact they have to be, the bound alone decides.
No kernel may reach another device: no remote copies, remote signals or barrier semaphores. Data moves between devices by JAX's collectives and lax.ppermute only.
A program may use at most 64 MiB of HBM per device.

v0:
```python
import functools
import math

import jax
import jax.numpy as jnp
from jax import lax
from jax.experimental import pallas as pl
from jax.experimental.pallas import tpu as pltpu
from jax.sharding import PartitionSpec as P

LANES = 128
SUB = 8
DENSE_LIMIT = 4 << 20
f32, bf16 = jnp.float32, jnp.bfloat16
VMEM = pl.BlockSpec(memory_space=pltpu.VMEM)
SMEM = pl.BlockSpec(memory_space=pltpu.SMEM)
NT = (((1,), (1,)), ((), ()))


def tile_terms(blocks, rows, cols, count, row_seg, col_seg):
    highest = lax.Precision.HIGHEST
    slots = blocks.shape[0]
    nvec = row_seg.shape[0]
    row_blocks = row_seg.shape[1] // blocks.shape[1]
    col_blocks = col_seg.shape[1] // blocks.shape[1]
    width = blocks.shape[1]
    live = (jnp.arange(slots, dtype=jnp.int32) < count).astype(jnp.float32)
    row_hits = (rows[:, None] == jnp.arange(row_blocks, dtype=jnp.int32)[None, :]).astype(jnp.float32) * live[:, None]
    col_hits = (cols[:, None] == jnp.arange(col_blocks, dtype=jnp.int32)[None, :]).astype(jnp.float32) * live[:, None]
    row_parts = row_seg.reshape(nvec, row_blocks, width)
    col_parts = col_seg.reshape(nvec, col_blocks, width)
    col_pick = jnp.take(col_parts, cols, axis=1)
    row_pick = jnp.take(row_parts, rows, axis=1)
    plain = jnp.einsum("kij,vkj->vki", blocks, col_pick, precision=highest)
    turned = jnp.einsum("kji,vkj->vki", blocks, row_pick, precision=highest)
    plain_part = jnp.einsum("kb,vki->vbi", row_hits, plain, precision=highest).reshape(nvec, row_blocks * width)
    turned_part = jnp.einsum("kb,vki->vbi", col_hits, turned, precision=highest).reshape(nvec, col_blocks * width)
    return plain_part, turned_part


def by_blocks(blk, vectors, values, block_rows, block_cols, counts):
    row_seg = lax.all_gather(vectors, "col", axis=1, tiled=True)
    col_seg = lax.all_gather(vectors, "row", axis=1, tiled=True)
    blocks = values.reshape(values.shape[0], blk, blk)
    plain, turned = tile_terms(blocks, block_rows[0], block_cols[0], counts[0, 0], row_seg, col_seg)
    plain = lax.psum_scatter(plain, "col", scatter_dimension=1, tiled=True)
    turned = lax.psum_scatter(turned, "row", scatter_dimension=1, tiled=True)
    return plain + turned


def build_kernel(blk, vectors, values, rows, cols, count, own, hi, lo, acc, held, row_of, col_of, sems):
    r, c = lax.axis_index("row"), lax.axis_index("col")
    half = blk // 2
    steps = half // SUB
    group = half * SUB
    groups = held.shape[0] // group
    small = [
        pltpu.make_async_copy(src, dst, sems.at[groups + i])
        for i, (src, dst) in enumerate(((rows, row_of), (cols, col_of), (vectors, own)))
    ]
    large = [
        pltpu.make_async_copy(values.at[pl.ds(g * group, group)], held.at[pl.ds(g * group, group)], sems.at[g])
        for g in range(groups)
    ]
    for copy in small + large:
        copy.start()
    acc[...] = jnp.zeros_like(acc)
    for copy in small:
        copy.wait()
    used = jnp.broadcast_to(count[...], (SUB, LANES))

    def add_slot(k, first):
        br = row_of[0, k] ^ (c * 2)
        bc = col_of[0, k] ^ (r * 2)
        for q in range(steps):
            piece = jnp.where(used > k, held[pl.ds(first + q * SUB * SUB, SUB, stride=SUB), :], 0.0)
            at = pl.multiple_of(br * half + q * SUB, SUB)
            acc[bc, pl.ds(at, SUB), :] += piece

    for g in range(groups):
        large[g].wait()
        for s in range(SUB):
            add_slot(g * SUB + s, g * group + s)
    for b in range(acc.shape[0]):
        dense = acc[b]
        top = dense.astype(bf16)
        hi[b] = top
        lo[b] = (dense - top.astype(f32)).astype(bf16)


def build(blk, nbr, nbc, vectors, values, block_rows, block_cols, counts):
    slots = values.shape[0]
    half = blk // 2
    view = values.reshape(slots // SUB, SUB, half, LANES).transpose(0, 2, 1, 3).reshape(slots * half, LANES)
    shape = (nbc, nbr * half, LANES)
    hbm = pl.BlockSpec(memory_space=pltpu.HBM)
    vectors, view, block_rows, block_cols = (
        pltpu.with_memory_space_constraint(x, pltpu.HBM) for x in (vectors, view, block_rows, block_cols)
    )
    return pl.pallas_call(
        functools.partial(build_kernel, blk),
        out_shape=[jax.ShapeDtypeStruct(vectors.shape, f32)] + [jax.ShapeDtypeStruct(shape, bf16)] * 2,
        in_specs=[hbm] * 4 + [VMEM],
        out_specs=[VMEM] * 3,
        scratch_shapes=[
            pltpu.VMEM(shape, f32),
            pltpu.VMEM(view.shape, f32),
            pltpu.SMEM(block_rows.shape, jnp.int32),
            pltpu.SMEM(block_cols.shape, jnp.int32),
            pltpu.SemaphoreType.DMA((slots // SUB + 3,)),
        ],
        compiler_params=pltpu.CompilerParams(vmem_limit_bytes=12 << 20),
        cost_estimate=pl.CostEstimate(flops=1 << 20, bytes_accessed=6 << 20, transcendentals=0),
        name="build",
    )(vectors, view, block_rows, block_cols, counts)


def split(x):
    top = x.astype(bf16).astype(f32)
    return jnp.concatenate([top, x - top], 0)


def fold():
    src = lax.broadcasted_iota(jnp.int32, (LANES, LANES), 0)
    dst = lax.broadcasted_iota(jnp.int32, (LANES, LANES), 1)
    half = LANES // 4
    want = ((dst // half) % 2) * (LANES // 2) + 2 * (dst % half) + dst // (LANES // 2)
    return (src == want).astype(f32).astype(bf16)


def low(rows):
    return lax.broadcasted_iota(jnp.int32, (rows, LANES), 1) < LANES // 2


def swap(x):
    return pltpu.roll(x, LANES // 2, 1)


def wide(ref, q):
    return jnp.concatenate([ref[2 * q], ref[2 * q + 1]], 1)


def load(refs):
    out = []
    for ref in refs:
        if len(ref.shape) == 2:
            out.append(ref[...])
        else:
            out += [ref[i] for i in range(ref.shape[0])]
    return out


def turned_kernel(nx, order, *refs):
    xs, (hi, lo), outs = load(refs[:nx]), refs[nx : nx + 2], refs[nx + 2 :]
    xs = [xs[k] for k in order]
    nv = xs[0].shape[0]
    folded = jnp.dot(jnp.concatenate([split(x) for x in xs], 0).astype(bf16), fold(), preferred_element_type=f32)
    m = low(2 * nv)
    even, odd = [], []
    for g in range(len(xs) // 2):
        a, b = folded[4 * nv * g : 4 * nv * g + 2 * nv], folded[4 * nv * g + 2 * nv : 4 * nv * g + 4 * nv]
        even.append(jnp.where(m, a, swap(b)))
        odd.append(jnp.where(m, swap(a), b))
    left = jnp.concatenate([jnp.concatenate(even, 1), jnp.concatenate(odd, 1)], 0).astype(bf16)
    m = low(nv)
    q = 0
    for out in outs:
        for i in range(out.shape[0]):
            t = jnp.dot(left, wide(hi, q), preferred_element_type=f32) + jnp.dot(left, wide(lo, q), preferred_element_type=f32)
            t0, t1 = t[:nv] + t[nv : 2 * nv], t[2 * nv : 3 * nv] + t[3 * nv :]
            out[i] = jnp.where(m, t0[:, :LANES] + swap(t1[:, :LANES]), swap(t0[:, LANES:]) + t1[:, LANES:])
            q += 1


def plain_kernel(nx, order, *refs):
    xs, (hi, lo), outs = load(refs[:nx]), refs[nx : nx + 2], refs[nx + 2 :]
    nv = xs[0].shape[0]
    m = low(2 * nv)
    total = None
    for q, x in enumerate(xs):
        s = split(x)
        r = swap(s)
        first = jnp.concatenate([jnp.where(m, s, 0.0), jnp.where(m, 0.0, r)], 0)
        second = jnp.concatenate([jnp.where(m, r, 0.0), jnp.where(m, 0.0, s)], 0)
        left = jnp.concatenate([first, second], 1).astype(bf16)
        t = lax.dot_general(left, wide(hi, q), NT, preferred_element_type=f32)
        t += lax.dot_general(left, wide(lo, q), NT, preferred_element_type=f32)
        total = t if total is None else total + t
    z0, z1 = total[:nv] + total[nv : 2 * nv], total[2 * nv : 3 * nv] + total[3 * nv :]
    m = low(nv)
    parts = []
    for g in range(z0.shape[1] // LANES):
        a, b = z0[:, LANES * g : LANES * (g + 1)], z1[:, LANES * g : LANES * (g + 1)]
        parts += [split(jnp.where(m, a, swap(b))), split(jnp.where(m, swap(a), b))]
    back = lax.dot_general(jnp.concatenate(parts, 0).astype(bf16), fold(), NT, preferred_element_type=f32)
    at = iter(order)
    for out in outs:
        for i in range(out.shape[0]):
            k = next(at)
            out[i] = back[2 * nv * k : 2 * nv * k + nv] + back[2 * nv * k + nv : 2 * nv * (k + 1)]


def call(kernel, xs, hi, lo, outs, order):
    nv = xs[0].shape[-2]
    return pl.pallas_call(
        functools.partial(kernel, len(xs), order),
        out_shape=[jax.ShapeDtypeStruct((n, nv, LANES), f32) for n in outs],
        in_specs=[VMEM] * (len(xs) + 2),
        out_specs=[VMEM] * len(outs),
        compiler_params=pltpu.CompilerParams(vmem_limit_bytes=12 << 20),
        cost_estimate=pl.CostEstimate(flops=1 << 26, bytes_accessed=2 << 20, transcendentals=0),
    )(*xs, hi, lo)


def turned_of(xs, hi, lo, outs, order):
    return call(turned_kernel, xs, hi, lo, outs, order)


def plain_of(xs, hi, lo, outs, order):
    return call(plain_kernel, xs, hi, lo, outs, order)


def trade(x, axis, step):
    n = lax.axis_size(axis)
    return lax.ppermute(x, axis, [(i, i ^ step) for i in range(n)])


def glue(body, ins, *outs):
    return pl.pallas_call(
        body,
        out_shape=[jax.ShapeDtypeStruct((n,) + ins[0].shape[-2:], f32) for n in outs],
        in_specs=[VMEM] * len(ins),
        out_specs=[VMEM] * len(outs),
        compiler_params=pltpu.CompilerParams(vmem_limit_bytes=1 << 20),
    )(*ins)


def join(*refs):
    out, at = refs[-1], 0
    for x in load(refs[:-1]):
        out[at] = x
        at += 1


def halve(a, b, keep, send):
    n = keep.shape[0]
    for i in range(n):
        keep[i] = a[i] + b[i]
        send[i] = a[n + i] + b[n + i]


def exchange(v, own, hi, lo):
    n1 = trade(v, "col", 1)
    n2 = trade(v, "col", 2)
    n3 = trade(v, "col", 3)
    x1 = trade(v, "row", 1)
    (s1,) = glue(join, [own, x1], 2)
    z1 = trade(s1, "row", 2)
    t0, t1 = turned_of([own, n1, n2, n3], hi, lo, (4, 4), (0, 1, 2, 3))
    far = trade(t1, "row", 4)
    (s2,) = glue(join, [s1, z1], 4)
    z2 = trade(s2, "row", 4)
    u0, u1 = glue(halve, [t0, far], 2, 2)
    mid = trade(u1, "row", 2)
    p0, p1 = plain_of([s2, z2], hi, lo, (2, 2), (0, 1, 3, 2))
    q0 = trade(p1, "col", 3)
    w0, w1 = glue(halve, [u0, mid], 1, 1)
    near = trade(w1, "row", 1)
    g0, g1 = glue(halve, [p0, q0], 1, 1)
    last = trade(g1, "col", 1)
    return (g0 + last + w0 + near)[0]


def solution(mesh):
    sizes = mesh.shape

    def per_device(vectors, values, block_rows, block_cols, counts):
        blk = math.isqrt(values.shape[1])
        piece = vectors.shape[1]
        nbr, nbc = sizes["col"] * piece // blk, sizes["row"] * piece // blk
        fits = nbr * nbc * blk * blk * 4 <= DENSE_LIMIT
        square = sizes["row"] == 8 and sizes["col"] == 4
        if not (fits and square and piece == LANES and 2 * blk == LANES and values.shape[0] % SUB == 0):
            return by_blocks(blk, vectors, values, block_rows, block_cols, counts)
        own, hi, lo = build(blk, nbr, nbc, vectors, values, block_rows, block_cols, counts)
        return exchange(vectors, own, hi, lo)

    spec = P("row", "col")
    return jax.shard_map(
        per_device,
        mesh=mesh,
        in_specs=(P(None, ("row", "col")), spec, spec, spec, spec),
        out_specs=P(None, ("row", "col")),
        check_vma=False,
    )
```

profile of v0, /device:TPU:0, one launch (start us, length us, event | category | flops | bytes accessed | tf_op | source)
XLA Modules:
  0.0 22.7 jit_solution(10781794539963850414)
XLA Ops:
  0.0 3.0 %collective-permute-start = (f32[8,128]{1,0:T(8,128)}, f32[8,128]{1,0:T(8,128)S(1)}, u32[]{:S(2)}, u32[]{:S(2)}) collective-permute-start(f32[8,128]{1,0:T(8,128)} %vectors.1), channel_id=1, source_target_pairs={{0,4},{4,0},{8,12},{12,8},{16,20},{20,16},{24,28},{28,24},{1,5},{5... | collective-permute-start | bytes 12296 | tf_op jit(solution)/shard_map/ppermute | solution.py:225
  3.0 0.0 collective-permute-start.5
  3.0 1.5 %collective-permute-start.6 = (f32[8,128]{1,0:T(8,128)}, f32[8,128]{1,0:T(8,128)S(1)}, u32[]{:S(2)}, u32[]{:S(2)}) collective-permute-start(f32[8,128]{1,0:T(8,128)} %vectors.1), channel_id=1, source_target_pairs={{0,2},{1,3},{2,0},{3,1},{4,6},{5,7},{6,4},{7,5},{8,10},{9,11},{10,... | collective-permute-start | bytes 12296 | tf_op jit(solution)/shard_map/ppermute | solution.py:225
  4.5 0.3 %collective-permute-start.7 = (f32[8,128]{1,0:T(8,128)}, f32[8,128]{1,0:T(8,128)S(1)}, u32[]{:S(2)}, u32[]{:S(2)}) collective-permute-start(f32[8,128]{1,0:T(8,128)} %vectors.1), channel_id=1, source_target_pairs={{0,3},{1,2},{2,1},{3,0},{4,7},{5,6},{6,5},{7,4},{8,11},{9,10},{10,... | collective-permute-start | bytes 12296 | tf_op jit(solution)/shard_map/ppermute | solution.py:225
  5.5 1.7 %build.1 = (f32[8,128]{1,0:T(8,128)S(1)}, bf16[16,256,128]{2,1,0:T(8,128)(2,1)S(1)}, bf16[16,256,128]{2,1,0:T(8,128)(2,1)S(1)}) custom-call(f32[8,128]{1,0:T(8,128)} %vectors.1, f32[2048,128]{1,0:T(8,128)} %bitcast.7, s32[1,64]{1,0:T(1,128)} %rows.1, s32[1,64]{1,0:T(1,128)} %cols.1, s32[1,1]{1,0:T(1,128)S(6)} %copy.6.count), custom_call_target="tpu_custom_call" | custom-call | flops 1048576 | bytes 6291456 | tf_op jit(solution)/shard_map/build/pallas_call | solution.py:100
  7.2 0.0 collective-permute-done.refs_1_
  7.2 1.6 %collective-permute-start.1 = (f32[2,8,128]{2,1,0:T(8,128)S(1)}, f32[2,8,128]{2,1,0:T(8,128)S(1)}, u32[]{:S(2)}, u32[]{:S(2)}) collective-permute-start(f32[2,8,128]{2,1,0:T(8,128)S(1)} %shard_map.55.refs_0_), channel_id=1, source_target_pairs={{0,8},{4,12},{8,0},{12,4},{16,24},{20,28},{24,16},{28,20},{1,9},{5... | collective-permute-start | bytes 24584 | tf_op jit(solution)/shard_map/ppermute | solution.py:225
  8.9 0.0 collective-permute-done.5.refs_1_
  8.9 0.0 collective-permute-done.6.refs_2_
  8.9 0.0 collective-permute-done.7.refs_3_
  8.9 0.7 %shard_map.59 = (f32[4,8,128]{2,1,0:T(8,128)S(1)}, f32[4,8,128]{2,1,0:T(8,128)S(1)}) custom-call(f32[8,128]{1,0:T(8,128)S(1)} %get-tuple-element.18.refs_0_, f32[8,128]{1,0:T(8,128)S(1)} %collective-permute-done.5.refs_1_, f32[8,128]{1,0:T(8,128)S(1)} %collective-permute-done.6.refs_2_, f32[8,128]{1,0:T(8,128)S(1)} %collective-permute-done.7.refs_3_, ...), custom_call_target="tpu_custom_call" | custom-call | flops 67108864 | bytes 2097152 | tf_op jit(solution)/shard_map/pallas_call | solution.py:205
  9.6 2.6 %collective-permute-start.8 = (f32[4,8,128]{2,1,0:T(8,128)S(1)}, f32[4,8,128]{2,1,0:T(8,128)S(1)}, u32[]{:S(2)}, u32[]{:S(2)}) collective-permute-start(f32[4,8,128]{2,1,0:T(8,128)S(1)} %get-tuple-element.26), channel_id=1, source_target_pairs={{0,16},{4,20},{8,24},{12,28},{16,0},{20,4},{24,8},{28,12},{1,17},{... | collective-permute-start | bytes 49160 | tf_op jit(solution)/shard_map/ppermute | solution.py:225
  12.2 0.0 collective-permute-done.1.refs_1_
  12.2 1.3 %collective-permute-start.2 = (f32[4,8,128]{2,1,0:T(8,128)S(1)}, f32[4,8,128]{2,1,0:T(8,128)S(1)}, u32[]{:S(2)}, u32[]{:S(2)}) collective-permute-start(f32[4,8,128]{2,1,0:T(8,128)S(1)} %shard_map.56.refs_0_), channel_id=1, source_target_pairs={{0,16},{4,20},{8,24},{12,28},{16,0},{20,4},{24,8},{28,12},{1,17},{... | collective-permute-start | bytes 49160 | tf_op jit(solution)/shard_map/ppermute | solution.py:225
  13.5 0.8 %collective-permute-done.8.b = f32[4,8,128]{2,1,0:T(8,128)S(1)} collective-permute-done((f32[4,8,128]{2,1,0:T(8,128)S(1)}, f32[4,8,128]{2,1,0:T(8,128)S(1)}, u32[]{:S(2)}, u32[]{:S(2)}) %collective-permute-start.8) | collective-permute-done | bytes 16416 | tf_op jit(solution)/shard_map/ppermute | solution.py:225
  14.3 0.8 %collective-permute-start.9 = (f32[2,8,128]{2,1,0:T(8,128)S(1)}, f32[2,8,128]{2,1,0:T(8,128)S(1)}, u32[]{:S(2)}, u32[]{:S(2)}) collective-permute-start(f32[2,8,128]{2,1,0:T(8,128)S(1)} %get-tuple-element.28), channel_id=1, source_target_pairs={{0,8},{4,12},{8,0},{12,4},{16,24},{20,28},{24,16},{28,20},{1,9},{5... | collective-permute-start | bytes 24584 | tf_op jit(solution)/shard_map/ppermute | solution.py:225
  15.2 1.7 %collective-permute-done.2.refs_1_ = f32[4,8,128]{2,1,0:T(8,128)S(1)} collective-permute-done((f32[4,8,128]{2,1,0:T(8,128)S(1)}, f32[4,8,128]{2,1,0:T(8,128)S(1)}, u32[]{:S(2)}, u32[]{:S(2)}) %collective-permute-start.2) | collective-permute-done | bytes 16416 | tf_op jit(solution)/shard_map/ppermute | solution.py:225
  16.9 0.9 %shard_map.57 = (f32[2,8,128]{2,1,0:T(8,128)S(1)}, f32[2,8,128]{2,1,0:T(8,128)S(1)}) custom-call(f32[4,8,128]{2,1,0:T(8,128)S(1)} %shard_map.56.refs_0_, f32[4,8,128]{2,1,0:T(8,128)S(1)} %collective-permute-done.2.refs_1_, bf16[16,256,128]{2,1,0:T(8,128)(2,1)S(1)} %get-tuple-element.19.refs_2_.refs_4_, ...), custom_call_target="tpu_custom_call" | custom-call | flops 67108864 | bytes 2097152 | tf_op jit(solution)/shard_map/pallas_call | solution.py:205
  17.8 0.0 collective-permute-start.3
  17.8 0.1 collective-permute-done.9.b
  18.0 0.5 %collective-permute-start.10 = (f32[1,8,128]{2,1,0:T(8,128)S(1)}, f32[1,8,128]{2,1,0:T(8,128)S(1)}, u32[]{:S(2)}, u32[]{:S(2)}) collective-permute-start(f32[1,8,128]{2,1,0:T(8,128)S(1)} %get-tuple-element.30), channel_id=1, source_target_pairs={{0,4},{4,0},{8,12},{12,8},{16,20},{20,16},{24,28},{28,24},{1,5},{5... | collective-permute-start | bytes 12296 | tf_op jit(solution)/shard_map/ppermute | solution.py:225
  18.5 2.4 %collective-permute-done.3.b = f32[2,8,128]{2,1,0:T(8,128)S(1)} collective-permute-done((f32[2,8,128]{2,1,0:T(8,128)S(1)}, f32[2,8,128]{2,1,0:T(8,128)S(1)}, u32[]{:S(2)}, u32[]{:S(2)}) %collective-permute-start.3) | collective-permute-done | bytes 8224 | tf_op jit(solution)/shard_map/ppermute | solution.py:225
  20.9 0.1 collective-permute-start.4
  21.0 0.5 %collective-permute-done.10 = f32[1,8,128]{2,1,0:T(8,128)S(1)} collective-permute-done((f32[1,8,128]{2,1,0:T(8,128)S(1)}, f32[1,8,128]{2,1,0:T(8,128)S(1)}, u32[]{:S(2)}, u32[]{:S(2)}) %collective-permute-start.10) | collective-permute-done | bytes 4128 | tf_op jit(solution)/shard_map/ppermute | solution.py:225
  21.6 0.5 %collective-permute-done.4 = f32[1,8,128]{2,1,0:T(8,128)S(1)} collective-permute-done((f32[1,8,128]{2,1,0:T(8,128)S(1)}, f32[1,8,128]{2,1,0:T(8,128)S(1)}, u32[]{:S(2)}, u32[]{:S(2)}) %collective-permute-start.4) | collective-permute-done | bytes 4128 | tf_op jit(solution)/shard_map/ppermute | solution.py:225
  22.1 0.6 %add_bitcast_fusion = f32[8,128]{1,0:T(8,128)} fusion(f32[1,8,128]{2,1,0:T(8,128)S(1)} %collective-permute-done.10, f32[1,8,128]{2,1,0:T(8,128)S(1)} %get-tuple-element.29, f32[1,8,128]{2,1,0:T(8,128)S(1)} %get-tuple-element.23, f32[1,8,128]{2,1,0:T(8,128)S(1)} %collective-permute-done.4), kind=kLoop, calls=%fused_computation | loop fusion | flops 3072 | bytes 20480 | tf_op jit(solution)/shard_map/squeeze | solution.py:271
  (5 shorter events, 0.0 us)
Async XLA Ops:
  0.0 7.2 %collective-permute-start = (f32[8,128]{1,0:T(8,128)}, f32[8,128]{1,0:T(8,128)S(1)}, u32[]{:S(2)}, u32[]{:S(2)}) collective-permute-start(f32[8,128]{1,0:T(8,128)} %vectors.1), channel_id=1, source_target_pairs={{0,4},{4,0},{8,12},{12,8},{16,20},{20,16},{24,28},{28,24},{1,5},{5... | collective-permute-start | bytes 12296 | tf_op jit(solution)/shard_map/ppermute | solution.py:225
  3.0 5.9 %collective-permute-start.5 = (f32[8,128]{1,0:T(8,128)}, f32[8,128]{1,0:T(8,128)S(1)}, u32[]{:S(2)}, u32[]{:S(2)}) collective-permute-start(f32[8,128]{1,0:T(8,128)} %vectors.1), channel_id=1, source_target_pairs={{0,1},{1,0},{2,3},{3,2},{4,5},{5,4},{6,7},{7,6},{8,9},{9,8},{10,11... | collective-permute-start | bytes 12296 | tf_op jit(solution)/shard_map/ppermute | solution.py:225
  3.0 5.9 %collective-permute-start.6 = (f32[8,128]{1,0:T(8,128)}, f32[8,128]{1,0:T(8,128)S(1)}, u32[]{:S(2)}, u32[]{:S(2)}) collective-permute-start(f32[8,128]{1,0:T(8,128)} %vectors.1), channel_id=1, source_target_pairs={{0,2},{1,3},{2,0},{3,1},{4,6},{5,7},{6,4},{7,5},{8,10},{9,11},{10,... | collective-permute-start | bytes 12296 | tf_op jit(solution)/shard_map/ppermute | solution.py:225
  4.5 4.4 %collective-permute-start.7 = (f32[8,128]{1,0:T(8,128)}, f32[8,128]{1,0:T(8,128)S(1)}, u32[]{:S(2)}, u32[]{:S(2)}) collective-permute-start(f32[8,128]{1,0:T(8,128)} %vectors.1), channel_id=1, source_target_pairs={{0,3},{1,2},{2,1},{3,0},{4,7},{5,6},{6,5},{7,4},{8,11},{9,10},{10,... | collective-permute-start | bytes 12296 | tf_op jit(solution)/shard_map/ppermute | solution.py:225
  7.2 5.0 %collective-permute-start.1 = (f32[2,8,128]{2,1,0:T(8,128)S(1)}, f32[2,8,128]{2,1,0:T(8,128)S(1)}, u32[]{:S(2)}, u32[]{:S(2)}) collective-permute-start(f32[2,8,128]{2,1,0:T(8,128)S(1)} %shard_map.55.refs_0_), channel_id=1, source_target_pairs={{0,8},{4,12},{8,0},{12,4},{16,24},{20,28},{24,16},{28,20},{1,9},{5... | collective-permute-start | bytes 24584 | tf_op jit(solution)/shard_map/ppermute | solution.py:225
  9.6 4.7 %collective-permute-start.8 = (f32[4,8,128]{2,1,0:T(8,128)S(1)}, f32[4,8,128]{2,1,0:T(8,128)S(1)}, u32[]{:S(2)}, u32[]{:S(2)}) collective-permute-start(f32[4,8,128]{2,1,0:T(8,128)S(1)} %get-tuple-element.26), channel_id=1, source_target_pairs={{0,16},{4,20},{8,24},{12,28},{16,0},{20,4},{24,8},{28,12},{1,17},{... | collective-permute-start | bytes 49160 | tf_op jit(solution)/shard_map/ppermute | solution.py:225
  12.2 4.7 %collective-permute-start.2 = (f32[4,8,128]{2,1,0:T(8,128)S(1)}, f32[4,8,128]{2,1,0:T(8,128)S(1)}, u32[]{:S(2)}, u32[]{:S(2)}) collective-permute-start(f32[4,8,128]{2,1,0:T(8,128)S(1)} %shard_map.56.refs_0_), channel_id=1, source_target_pairs={{0,16},{4,20},{8,24},{12,28},{16,0},{20,4},{24,8},{28,12},{1,17},{... | collective-permute-start | bytes 49160 | tf_op jit(solution)/shard_map/ppermute | solution.py:225
  14.3 3.7 %collective-permute-start.9 = (f32[2,8,128]{2,1,0:T(8,128)S(1)}, f32[2,8,128]{2,1,0:T(8,128)S(1)}, u32[]{:S(2)}, u32[]{:S(2)}) collective-permute-start(f32[2,8,128]{2,1,0:T(8,128)S(1)} %get-tuple-element.28), channel_id=1, source_target_pairs={{0,8},{4,12},{8,0},{12,4},{16,24},{20,28},{24,16},{28,20},{1,9},{5... | collective-permute-start | bytes 24584 | tf_op jit(solution)/shard_map/ppermute | solution.py:225
  17.8 3.1 %collective-permute-start.3 = (f32[2,8,128]{2,1,0:T(8,128)S(1)}, f32[2,8,128]{2,1,0:T(8,128)S(1)}, u32[]{:S(2)}, u32[]{:S(2)}) collective-permute-start(f32[2,8,128]{2,1,0:T(8,128)S(1)} %get-tuple-element.22), channel_id=1, source_target_pairs={{0,3},{1,2},{2,1},{3,0},{4,7},{5,6},{6,5},{7,4},{8,11},{9,10},{10,... | collective-permute-start | bytes 24584 | tf_op jit(solution)/shard_map/ppermute | solution.py:225
  18.0 3.6 %collective-permute-start.10 = (f32[1,8,128]{2,1,0:T(8,128)S(1)}, f32[1,8,128]{2,1,0:T(8,128)S(1)}, u32[]{:S(2)}, u32[]{:S(2)}) collective-permute-start(f32[1,8,128]{2,1,0:T(8,128)S(1)} %get-tuple-element.30), channel_id=1, source_target_pairs={{0,4},{4,0},{8,12},{12,8},{16,20},{20,16},{24,28},{28,24},{1,5},{5... | collective-permute-start | bytes 12296 | tf_op jit(solution)/shard_map/ppermute | solution.py:225
  20.9 1.2 %collective-permute-start.4 = (f32[1,8,128]{2,1,0:T(8,128)S(1)}, f32[1,8,128]{2,1,0:T(8,128)S(1)}, u32[]{:S(2)}, u32[]{:S(2)}) collective-permute-start(f32[1,8,128]{2,1,0:T(8,128)S(1)} %get-tuple-element.24), channel_id=1, source_target_pairs={{0,1},{1,0},{2,3},{3,2},{4,5},{5,4},{6,7},{7,6},{8,9},{9,8},{10,11... | collective-permute-start | bytes 12296 | tf_op jit(solution)/shard_map/ppermute | solution.py:225
where the time goes:
time: 22.8 us; the launch traced here: 22.7 us
  starting transfers between devices  11.9 us (52%)
  waiting for transfers between devices  6.17 us (27%)
  Pallas kernels  3.36 us (15%)
  between operations  0.69 us (3%)
  other arithmetic  0.6 us (3%)
    ppermute x11, starting transfers between devices, trade(): return lax.ppermute(x, axis, [(i, i ^ step) for i in range(n)])  11.9 us
    ppermute x11, waiting for transfers between devices, trade(): return lax.ppermute(x, axis, [(i, i ^ step) for i in range(n)])  6.17 us
    pallas_call x1, Pallas kernels, build(): pl.pallas_call(functools.partial(build_kernel, blk), out_shape=[jax.Shape...  1.71 us
    pallas_call x2, Pallas kernels, call(): pl.pallas_call(functools.partial(kernel, len(xs), order), out_shape=[jax....  1.63 us
    squeeze x1, other arithmetic, exchange(): return (g0 + last + w0 + near)[0]  0.6 us
  transfers between devices with their start and end apart: 11, of which 6 were waited for; matrix products, arithmetic and copies ran while one was open for 0% of the time, Pallas kernels for 15%

commit v1 on v0

v1 whole, which is shorter than its diff:
```python
import functools
import math

import jax
import jax.numpy as jnp
from jax import lax
from jax.experimental import pallas as pl
from jax.experimental.pallas import tpu as pltpu
from jax.sharding import PartitionSpec as P

LANES = 128
SUB = 8
DENSE_LIMIT = 4 << 20
f32, bf16 = jnp.float32, jnp.bfloat16
VMEM = pl.BlockSpec(memory_space=pltpu.VMEM)
SMEM = pl.BlockSpec(memory_space=pltpu.SMEM)
NT = (((1,), (1,)), ((), ()))


def tile_terms(blocks, rows, cols, count, row_seg, col_seg):
    highest = lax.Precision.HIGHEST
    slots = blocks.shape[0]
    nvec = row_seg.shape[0]
    row_blocks = row_seg.shape[1] // blocks.shape[1]
    col_blocks = col_seg.shape[1] // blocks.shape[1]
    width = blocks.shape[1]
    live = (jnp.arange(slots, dtype=jnp.int32) < count).astype(jnp.float32)
    row_hits = (rows[:, None] == jnp.arange(row_blocks, dtype=jnp.int32)[None, :]).astype(jnp.float32) * live[:, None]
    col_hits = (cols[:, None] == jnp.arange(col_blocks, dtype=jnp.int32)[None, :]).astype(jnp.float32) * live[:, None]
    row_parts = row_seg.reshape(nvec, row_blocks, width)
    col_parts = col_seg.reshape(nvec, col_blocks, width)
    col_pick = jnp.take(col_parts, cols, axis=1)
    row_pick = jnp.take(row_parts, rows, axis=1)
    plain = jnp.einsum("kij,vkj->vki", blocks, col_pick, precision=highest)
    turned = jnp.einsum("kji,vkj->vki", blocks, row_pick, precision=highest)
    plain_part = jnp.einsum("kb,vki->vbi", row_hits, plain, precision=highest).reshape(nvec, row_blocks * width)
    turned_part = jnp.einsum("kb,vki->vbi", col_hits, turned, precision=highest).reshape(nvec, col_blocks * width)
    return plain_part, turned_part


def by_blocks(blk, vectors, values, block_rows, block_cols, counts):
    row_seg = lax.all_gather(vectors, "col", axis=1, tiled=True)
    col_seg = lax.all_gather(vectors, "row", axis=1, tiled=True)
    blocks = values.reshape(values.shape[0], blk, blk)
    plain, turned = tile_terms(blocks, block_rows[0], block_cols[0], counts[0, 0], row_seg, col_seg)
    plain = lax.psum_scatter(plain, "col", scatter_dimension=1, tiled=True)
    turned = lax.psum_scatter(turned, "row", scatter_dimension=1, tiled=True)
    return plain + turned


def init_kernel(acc):
    acc[...] = jnp.zeros_like(acc)


def build_kernel(blk, values, rows, cols, count, start, hi, lo, acc):
    del start
    r, c = lax.axis_index("row"), lax.axis_index("col")
    half = blk // 2
    steps = half // SUB
    group = half * SUB
    used = jnp.broadcast_to(count[...], (SUB, LANES))
    side = lax.broadcasted_iota(jnp.int32, (SUB, LANES), 1) // blk

    def add_slot(k, first):
        br = rows[0, k] ^ (c * 2)
        bc = cols[0, k] ^ (r * 2)
        q, odd = bc // 2, bc % 2
        keep = (side == odd) & (used > k)
        swapped = jnp.broadcast_to(odd, (SUB, LANES)) == 1
        for s in range(steps):
            two = values[pl.ds(first + s * SUB * SUB, SUB, stride=SUB), :]
            turn = swap(two)
            at = br * blk + 2 * SUB * s
            acc[q, pl.ds(at, SUB, stride=2), :] += jnp.where(keep, jnp.where(swapped, turn, two), 0.0)
            acc[q, pl.ds(at + 1, SUB, stride=2), :] += jnp.where(keep, jnp.where(swapped, two, turn), 0.0)

    for k in range(values.shape[0] // half):
        add_slot(k, k // SUB * group + k % SUB)
    for q in range(acc.shape[0]):
        dense = acc[q]
        top = dense.astype(bf16)
        hi[q] = top
        lo[q] = (dense - top.astype(f32)).astype(bf16)


def build(blk, nbr, nbc, vectors, values, block_rows, block_cols, counts):
    slots = values.shape[0]
    half = blk // 2
    view = values.reshape(slots // SUB, SUB, half, LANES).transpose(0, 2, 1, 3).reshape(slots * half, LANES)
    shape = (nbc // 2, nbr * blk, LANES)
    start = pl.pallas_call(
        init_kernel,
        out_shape=jax.ShapeDtypeStruct(shape, f32),
        out_specs=VMEM,
        compiler_params=pltpu.CompilerParams(vmem_limit_bytes=4 << 20),
        cost_estimate=pl.CostEstimate(flops=1 << 20, bytes_accessed=2 << 20, transcendentals=0),
        name="init",
    )()
    hi, lo, _ = pl.pallas_call(
        functools.partial(build_kernel, blk),
        out_shape=[jax.ShapeDtypeStruct(shape, bf16)] * 2 + [jax.ShapeDtypeStruct(shape, f32)],
        in_specs=[VMEM, SMEM, SMEM, VMEM, VMEM],
        out_specs=[VMEM] * 3,
        input_output_aliases={4: 2},
        compiler_params=pltpu.CompilerParams(vmem_limit_bytes=12 << 20),
        cost_estimate=pl.CostEstimate(flops=1 << 20, bytes_accessed=6 << 20, transcendentals=0),
        name="build",
    )(view, block_rows, block_cols, counts, start)
    return vectors, hi, lo


def split(x):
    top = x.astype(bf16).astype(f32)
    return jnp.concatenate([top, x - top], 0)


def swap(x):
    return pltpu.roll(x, LANES // 2, 1)


def wide(ref, q):
    return jnp.concatenate([ref[q], ref[q + 1]], 1)


def load(refs):
    out = []
    for ref in refs:
        if len(ref.shape) == 2:
            out.append(ref[...])
        else:
            out += [ref[i] for i in range(ref.shape[0])]
    return out


def pieces(refs, names):
    return dict(zip(names, load(refs), strict=True))


def places(refs, names):
    return dict(zip(names, ((ref, i) for ref in refs for i in range(ref.shape[0])), strict=True))


def turned_kernel(nx, take, put, *refs):
    xs, (hi, lo), outs = pieces(refs[:nx], take), refs[nx : nx + 2], places(refs[nx + 2 :], put)
    nv = xs[0].shape[0]
    left = jnp.concatenate([split(xs[k]) for k in range(len(xs))], 1).astype(bf16)
    for q in range(0, len(outs), 2):
        t = jnp.dot(left, wide(hi, q), preferred_element_type=f32) + jnp.dot(left, wide(lo, q), preferred_element_type=f32)
        t = t[:nv] + t[nv:]
        for i in range(2):
            out, at = outs[q + i]
            out[at] = t[:, LANES * i : LANES * (i + 1)]


def plain_kernel(nx, take, put, *refs):
    xs, (hi, lo), outs = pieces(refs[:nx], take), refs[nx : nx + 2], places(refs[nx + 2 :], put)
    nv = xs[0].shape[0]
    total = 0.0
    for q in range(0, len(xs), 2):
        left = jnp.concatenate([split(xs[q]), split(xs[q + 1])], 1).astype(bf16)
        for part in (hi, lo):
            total += lax.dot_general(left, wide(part, q), NT, preferred_element_type=f32)
    total = total[:nv] + total[nv:]
    for k, (out, at) in outs.items():
        out[at] = total[:, LANES * k : LANES * (k + 1)]


def call(kernel, xs, hi, lo, outs, take, put):
    nv = xs[0].shape[-2]
    return pl.pallas_call(
        functools.partial(kernel, len(xs), take, put),
        out_shape=[jax.ShapeDtypeStruct((n, nv, LANES), f32) for n in outs],
        in_specs=[VMEM] * (len(xs) + 2),
        out_specs=[VMEM] * len(outs),
        compiler_params=pltpu.CompilerParams(vmem_limit_bytes=12 << 20),
        cost_estimate=pl.CostEstimate(flops=1 << 26, bytes_accessed=2 << 20, transcendentals=0),
    )(*xs, hi, lo)


def turned_of(xs, hi, lo, outs, take, put):
    return call(turned_kernel, xs, hi, lo, outs, take, put)


def plain_of(xs, hi, lo, outs, take, put):
    return call(plain_kernel, xs, hi, lo, outs, take, put)


def trade(x, axis, step):
    n = lax.axis_size(axis)
    return lax.ppermute(x, axis, [(i, i ^ step) for i in range(n)])


def glue(body, ins, *outs):
    return pl.pallas_call(
        body,
        out_shape=[jax.ShapeDtypeStruct((n,) + ins[0].shape[-2:], f32) for n in outs],
        in_specs=[VMEM] * len(ins),
        out_specs=[VMEM] * len(outs),
        compiler_params=pltpu.CompilerParams(vmem_limit_bytes=1 << 20),
    )(*ins)


def join(*refs):
    out, at = refs[-1], 0
    for x in load(refs[:-1]):
        out[at] = x
        at += 1


def halve(a, b, keep, send):
    n = keep.shape[0]
    for i in range(n):
        keep[i] = a[i] + b[i]
        send[i] = a[n + i] + b[n + i]


def add_parts(a, b, *outs):
    for i, out in enumerate(outs):
        out[0] = a[i] + b[i]


def exchange(v, hi, lo):
    n1 = trade(v, "col", 1)
    (c1,) = glue(join, [v, n1], 2)
    n2 = trade(c1, "col", 3)
    t0, t1 = turned_of([c1, n2], hi, lo, (4, 4), (0, 1, 3, 2), (0, 2, 4, 6, 1, 3, 5, 7))
    x1 = trade(v, "row", 2)
    (s1,) = glue(join, [v, x1], 2)
    z1 = trade(s1, "row", 1)
    (s2,) = glue(join, [s1, z1], 4)
    z2 = trade(s2, "row", 4)
    p0, p1 = plain_of([s2, z2], hi, lo, (2, 2), (0, 2, 1, 3, 4, 6, 5, 7), (0, 1, 3, 2))
    u0, u2, u4, u6 = glue(add_parts, [t0, trade(t1, "row", 1)], 1, 1, 1, 1)
    w = u0 + trade(u2, "row", 2) + trade(u4, "row", 4) + trade(u6, "row", 6)
    q0 = trade(p1, "col", 3)
    g0, g1 = glue(halve, [p0, q0], 1, 1)
    last = trade(g1, "col", 1)
    return (g0 + last + w)[0]


def solution(mesh):
    sizes = mesh.shape

    def per_device(vectors, values, block_rows, block_cols, counts):
        blk = math.isqrt(values.shape[1])
        piece = vectors.shape[1]
        nbr, nbc = sizes["col"] * piece // blk, sizes["row"] * piece // blk
        fits = nbr * nbc * blk * blk * 4 <= DENSE_LIMIT
        square = sizes["row"] == 8 and sizes["col"] == 4
        if not (fits and square and piece == LANES and 2 * blk == LANES and values.shape[0] % SUB == 0):
            return by_blocks(blk, vectors, values, block_rows, block_cols, counts)
        _, hi, lo = build(blk, nbr, nbc, vectors, values, block_rows, block_cols, counts)
        return exchange(vectors, hi, lo)

    spec = P("row", "col")
    return jax.shard_map(
        per_device,
        mesh=mesh,
        in_specs=(P(None, ("row", "col")), spec, spec, spec, spec),
        out_specs=P(None, ("row", "col")),
        check_vma=False,
    )
```

time: 22.8 us -> 26.4 us (1.16)
  starting transfers between devices: 11.9 us -> 14.5 us
  waiting for transfers between devices: 6.17 us -> 7.12 us
  Pallas kernels: 3.36 us -> 2.65 us
  local copies, waits for them, and re-layouts: 0 us -> 0.7 us
    ppermute x11, starting transfers between devices: 11.9 us -> 14.5 us  [trade(): return lax.ppermute(x, axis, [(i, i ^ step) for i in range(n)])]
    ppermute x11, waiting for transfers between devices: 6.17 us -> 7.12 us  [trade(): return lax.ppermute(x, axis, [(i, i ^ step) for i in range(n)])]
    unnamed x0 -> x8, local copies, waits for them, and re-layouts: none -> 0.7 us
    pallas_call x2 -> x3, Pallas kernels: 1.63 us -> 1.16 us  [the longest x2 1.02 us: call(): pl.pallas_call(functools.partial(kernel, len(xs), take, put), out_shape=[...]
  transfers between devices with their start and end apart: 11 -> 11, of which waited for: 6 -> 6; matrix products, arithmetic and copies ran while one was open for 0% -> 0% of each run, Pallas kernels for 15% -> 10%
where the time goes in v1:
time: 26.4 us; the launch traced here: 26.3 us
  starting transfers between devices  14.5 us (55%)
  waiting for transfers between devices  7.12 us (27%)
  Pallas kernels  2.65 us (10%)
  between operations  0.72 us (3%)
  local copies, waits for them, and re-layouts  0.7 us (3%)
  other arithmetic  0.6 us (2%)
    ppermute x11, starting transfers between devices, trade(): return lax.ppermute(x, axis, [(i, i ^ step) for i in range(n)])  14.5 us
    ppermute x11, waiting for transfers between devices, trade(): return lax.ppermute(x, axis, [(i, i ^ step) for i in range(n)])  7.12 us
    pallas_call x1, Pallas kernels, build(): pl.pallas_call(functools.partial(build_kernel, blk), out_shape=[jax.Shape...  1.48 us
    pallas_call x2, Pallas kernels, call(): pl.pallas_call(functools.partial(kernel, len(xs), take, put), out_shape=[...  1.02 us
    unnamed x8, local copies, waits for them, and re-layouts  0.7 us
    squeeze x1, other arithmetic, exchange(): return (g0 + last + w)[0]  0.6 us
  transfers between devices with their start and end apart: 11, of which 6 were waited for; matrix products, arithmetic and copies ran while one was open for 0% of the time, Pallas kernels for 10%

profile of v1, /device:TPU:0, one launch (start us, length us, event | category | flops | bytes accessed | tf_op | source)
XLA Modules:
  0.0 26.3 jit_solution(16914749311274823930)
XLA Ops:
  0.0 0.0 copy-start
  0.0 3.1 %collective-permute-start = (f32[8,128]{1,0:T(8,128)}, f32[8,128]{1,0:T(8,128)S(1)}, u32[]{:S(2)}, u32[]{:S(2)}) collective-permute-start(f32[8,128]{1,0:T(8,128)} %refs_0_.3), channel_id=1, source_target_pairs={{0,8},{4,12},{8,0},{12,4},{16,24},{20,28},{24,16},{28,20},{1,9},{5... | collective-permute-start | bytes 12296 | tf_op jit(solution)/shard_map/ppermute | solution.py:190
  3.1 1.8 %collective-permute-done.refs_1_ = f32[8,128]{1,0:T(8,128)S(1)} collective-permute-done((f32[8,128]{1,0:T(8,128)}, f32[8,128]{1,0:T(8,128)S(1)}, u32[]{:S(2)}, u32[]{:S(2)}) %collective-permute-start) | collective-permute-done | bytes 4128 | tf_op jit(solution)/shard_map/ppermute | solution.py:190
  4.8 0.0 copy-start.1
  4.9 0.7 %copy-done.1 = f32[8,128]{1,0:T(8,128)S(1)} copy-done((f32[8,128]{1,0:T(8,128)S(1)}, f32[8,128]{1,0:T(8,128)}, u32[]{:S(2)}) %copy-start.1) | copy-done | bytes 4120
  5.5 0.0 copy-start.2
  5.5 0.0 copy-start.3
  5.5 1.9 %collective-permute-start.1 = (f32[2,8,128]{2,1,0:T(8,128)S(1)}, f32[2,8,128]{2,1,0:T(8,128)S(1)}, u32[]{:S(2)}, u32[]{:S(2)}) collective-permute-start(f32[2,8,128]{2,1,0:T(8,128)S(1)} %shard_map.55.refs_0_), channel_id=1, source_target_pairs={{0,4},{4,0},{8,12},{12,8},{16,20},{20,16},{24,28},{28,24},{1,5},{5... | collective-permute-start | bytes 24584 | tf_op jit(solution)/shard_map/ppermute | solution.py:190
  7.5 0.0 collective-permute-start.5
  7.5 1.2 %collective-permute-done.5.refs_1_ = f32[8,128]{1,0:T(8,128)S(1)} collective-permute-done((f32[8,128]{1,0:T(8,128)S(1)}, f32[8,128]{1,0:T(8,128)S(1)}, u32[]{:S(2)}, u32[]{:S(2)}) %collective-permute-start.5) | collective-permute-done | bytes 4128 | tf_op jit(solution)/shard_map/ppermute | solution.py:190
  8.7 1.3 %collective-permute-start.6 = (f32[2,8,128]{2,1,0:T(8,128)S(1)}, f32[2,8,128]{2,1,0:T(8,128)S(1)}, u32[]{:S(2)}, u32[]{:S(2)}) collective-permute-start(f32[2,8,128]{2,1,0:T(8,128)S(1)} %shard_map.59.refs_0_), channel_id=1, source_target_pairs={{0,3},{1,2},{2,1},{3,0},{4,7},{5,6},{6,5},{7,4},{8,11},{9,10},{10,... | collective-permute-start | bytes 24584 | tf_op jit(solution)/shard_map/ppermute | solution.py:190
  9.9 0.0 collective-permute-done.1.refs_1_
  10.0 2.6 %collective-permute-start.2 = (f32[4,8,128]{2,1,0:T(8,128)S(1)}, f32[4,8,128]{2,1,0:T(8,128)S(1)}, u32[]{:S(2)}, u32[]{:S(2)}) collective-permute-start(f32[4,8,128]{2,1,0:T(8,128)S(1)} %shard_map.56.refs_0_), channel_id=1, source_target_pairs={{0,16},{4,20},{8,24},{12,28},{16,0},{20,4},{24,8},{28,12},{1,17},{... | collective-permute-start | bytes 49160 | tf_op jit(solution)/shard_map/ppermute | solution.py:190
  13.2 0.1 init.1.start
  13.3 0.0 copy-done
  13.3 0.0 copy-done.2
  13.4 0.0 copy-done.3
  13.4 1.5 %build.1 = (bf16[8,512,128]{2,1,0:T(8,128)(2,1)S(1)}, bf16[8,512,128]{2,1,0:T(8,128)(2,1)S(1)}, f32[8,512,128]{2,1,0:T(8,128)S(1)}) custom-call(f32[2048,128]{1,0:T(8,128)S(1)} %bitcast.7, s32[1,64]{1,0:T(1,128)S(1)} %copy-done.2, s32[1,64]{1,0:T(1,128)S(1)} %copy-done.3, s32[1,1]{1,0:T(1,128)S(6)} %copy.8.count, ...), custom_call_target="tpu_custom_call", output_to_operand_aliasing={{2}: (4, {})} | custom-call | flops 1048576 | bytes 6291456 | tf_op jit(solution)/shard_map/build/pallas_call | solution.py:99
  14.9 0.0 collective-permute-done.6.refs_1_
  14.9 0.4 %shard_map.60 = (f32[4,8,128]{2,1,0:T(8,128)S(1)}, f32[4,8,128]{2,1,0:T(8,128)S(1)}) custom-call(f32[2,8,128]{2,1,0:T(8,128)S(1)} %shard_map.59.refs_0_, f32[2,8,128]{2,1,0:T(8,128)S(1)} %collective-permute-done.6.refs_1_, bf16[8,512,128]{2,1,0:T(8,128)(2,1)S(1)} %get-tuple-element.17.refs_2_, bf16[8,512,128]{2,1,0:T(8,128)(2,1)S(1)} %get-tuple-element.18.refs_3_), custom_call_target="tpu_custom_call" | custom-call | flops 67108864 | bytes 2097152 | tf_op jit(solution)/shard_map/pallas_call | solution.py:170
  15.2 1.2 %collective-permute-start.7 = (f32[4,8,128]{2,1,0:T(8,128)S(1)}, f32[4,8,128]{2,1,0:T(8,128)S(1)}, u32[]{:S(2)}, u32[]{:S(2)}) collective-permute-start(f32[4,8,128]{2,1,0:T(8,128)S(1)} %get-tuple-element.24), channel_id=1, source_target_pairs={{0,4},{4,0},{8,12},{12,8},{16,20},{20,16},{24,28},{28,24},{1,5},{5... | collective-permute-start | bytes 49160 | tf_op jit(solution)/shard_map/ppermute | solution.py:190
  16.4 0.0 collective-permute-done.2.refs_1_
  16.4 0.6 %shard_map.57 = (f32[2,8,128]{2,1,0:T(8,128)S(1)}, f32[2,8,128]{2,1,0:T(8,128)S(1)}) custom-call(f32[4,8,128]{2,1,0:T(8,128)S(1)} %shard_map.56.refs_0_, f32[4,8,128]{2,1,0:T(8,128)S(1)} %collective-permute-done.2.refs_1_, bf16[8,512,128]{2,1,0:T(8,128)(2,1)S(1)} %get-tuple-element.17.refs_2_, bf16[8,512,128]{2,1,0:T(8,128)(2,1)S(1)} %get-tuple-element.18.refs_3_), custom_call_target="tpu_custom_call" | custom-call | flops 67108864 | bytes 2097152 | tf_op jit(solution)/shard_map/pallas_call | solution.py:170
  17.1 0.0 collective-permute-start.3
  17.1 1.9 %collective-permute-done.7.b = f32[4,8,128]{2,1,0:T(8,128)S(1)} collective-permute-done((f32[4,8,128]{2,1,0:T(8,128)S(1)}, f32[4,8,128]{2,1,0:T(8,128)S(1)}, u32[]{:S(2)}, u32[]{:S(2)}) %collective-permute-start.7) | collective-permute-done | bytes 16416 | tf_op jit(solution)/shard_map/ppermute | solution.py:190
  19.0 1.3 %collective-permute-start.10 = (f32[1,8,128]{2,1,0:T(8,128)S(1)}, f32[1,8,128]{2,1,0:T(8,128)S(1)}, u32[]{:S(2)}, u32[]{:S(2)}) collective-permute-start(f32[1,8,128]{2,1,0:T(8,128)S(1)} %get-tuple-element.28), channel_id=1, source_target_pairs={{0,24},{4,28},{8,16},{12,20},{16,8},{20,12},{24,0},{28,4},{1,25},{... | collective-permute-start | bytes 12296 | tf_op jit(solution)/shard_map/ppermute | solution.py:190
  20.3 1.7 %collective-permute-start.9 = (f32[1,8,128]{2,1,0:T(8,128)S(1)}, f32[1,8,128]{2,1,0:T(8,128)S(1)}, u32[]{:S(2)}, u32[]{:S(2)}) collective-permute-start(f32[1,8,128]{2,1,0:T(8,128)S(1)} %get-tuple-element.27), channel_id=1, source_target_pairs={{0,16},{4,20},{8,24},{12,28},{16,0},{20,4},{24,8},{28,12},{1,17},{... | collective-permute-start | bytes 12296 | tf_op jit(solution)/shard_map/ppermute | solution.py:190
  22.0 1.3 %collective-permute-start.8 = (f32[1,8,128]{2,1,0:T(8,128)S(1)}, f32[1,8,128]{2,1,0:T(8,128)S(1)}, u32[]{:S(2)}, u32[]{:S(2)}) collective-permute-start(f32[1,8,128]{2,1,0:T(8,128)S(1)} %get-tuple-element.26), channel_id=1, source_target_pairs={{0,8},{4,12},{8,0},{12,4},{16,24},{20,28},{24,16},{28,20},{1,9},{5... | collective-permute-start | bytes 12296 | tf_op jit(solution)/shard_map/ppermute | solution.py:190
  23.4 0.0 collective-permute-done.3.b
  23.4 0.0 collective-permute-start.4
  23.4 1.0 %collective-permute-done.10 = f32[1,8,128]{2,1,0:T(8,128)S(1)} collective-permute-done((f32[1,8,128]{2,1,0:T(8,128)S(1)}, f32[1,8,128]{2,1,0:T(8,128)S(1)}, u32[]{:S(2)}, u32[]{:S(2)}) %collective-permute-start.10) | collective-permute-done | bytes 4128 | tf_op jit(solution)/shard_map/ppermute | solution.py:190
  24.4 0.4 %collective-permute-done.9 = f32[1,8,128]{2,1,0:T(8,128)S(1)} collective-permute-done((f32[1,8,128]{2,1,0:T(8,128)S(1)}, f32[1,8,128]{2,1,0:T(8,128)S(1)}, u32[]{:S(2)}, u32[]{:S(2)}) %collective-permute-start.9) | collective-permute-done | bytes 4128 | tf_op jit(solution)/shard_map/ppermute | solution.py:190
  24.9 0.8 %collective-permute-done.8 = f32[1,8,128]{2,1,0:T(8,128)S(1)} collective-permute-done((f32[1,8,128]{2,1,0:T(8,128)S(1)}, f32[1,8,128]{2,1,0:T(8,128)S(1)}, u32[]{:S(2)}, u32[]{:S(2)}) %collective-permute-start.8) | collective-permute-done | bytes 4128 | tf_op jit(solution)/shard_map/ppermute | solution.py:190
  25.6 0.0 collective-permute-done.4
  25.7 0.6 %add_bitcast_fusion = f32[8,128]{1,0:T(8,128)} fusion(f32[1,8,128]{2,1,0:T(8,128)S(1)} %collective-permute-done.10, f32[1,8,128]{2,1,0:T(8,128)S(1)} %collective-permute-done.9, f32[1,8,128]{2,1,0:T(8,128)S(1)} %get-tuple-element.25, f32[1,8,128]{2,1,0:T(8,128)S(1)} %collective-permute-done.8, f32[1,8,128]{2,1,0:T(8,128)S(1)} %get-tuple-element.21, ...), kind=kLoop, calls=%fused_computation | loop fusion | flops 5120 | bytes 28672 | tf_op jit(solution)/shard_map/squeeze | solution.py:238
  (5 shorter events, 0.0 us)
Async XLA Ops:
  0.0 13.3 %copy-start = (f32[64,4096]{1,0:T(8,128)S(1)}, f32[64,4096]{1,0:T(8,128)}, u32[]{:S(2)}) copy-start(f32[64,4096]{1,0:T(8,128)} %param.6) | copy-start | bytes 3145732
  0.0 4.8 %collective-permute-start = (f32[8,128]{1,0:T(8,128)}, f32[8,128]{1,0:T(8,128)S(1)}, u32[]{:S(2)}, u32[]{:S(2)}) collective-permute-start(f32[8,128]{1,0:T(8,128)} %refs_0_.3), channel_id=1, source_target_pairs={{0,8},{4,12},{8,0},{12,4},{16,24},{20,28},{24,16},{28,20},{1,9},{5... | collective-permute-start | bytes 12296 | tf_op jit(solution)/shard_map/ppermute | solution.py:190
  4.8 0.7 %copy-start.1 = (f32[8,128]{1,0:T(8,128)S(1)}, f32[8,128]{1,0:T(8,128)}, u32[]{:S(2)}) copy-start(f32[8,128]{1,0:T(8,128)} %refs_0_.3) | copy-start | bytes 12292
  5.5 7.8 %copy-start.2 = (s32[1,64]{1,0:T(1,128)S(1)}, s32[1,64]{1,0:T(1,128)}, u32[]{:S(2)}) copy-start(s32[1,64]{1,0:T(1,128)} %rows.1) | copy-start | bytes 772
  5.5 7.8 %copy-start.3 = (s32[1,64]{1,0:T(1,128)S(1)}, s32[1,64]{1,0:T(1,128)}, u32[]{:S(2)}) copy-start(s32[1,64]{1,0:T(1,128)} %cols.1) | copy-start | bytes 772
  5.5 4.4 %collective-permute-start.1 = (f32[2,8,128]{2,1,0:T(8,128)S(1)}, f32[2,8,128]{2,1,0:T(8,128)S(1)}, u32[]{:S(2)}, u32[]{:S(2)}) collective-permute-start(f32[2,8,128]{2,1,0:T(8,128)S(1)} %shard_map.55.refs_0_), channel_id=1, source_target_pairs={{0,4},{4,0},{8,12},{12,8},{16,20},{20,16},{24,28},{28,24},{1,5},{5... | collective-permute-start | bytes 24584 | tf_op jit(solution)/shard_map/ppermute | solution.py:190
  7.5 1.2 %collective-permute-start.5 = (f32[8,128]{1,0:T(8,128)S(1)}, f32[8,128]{1,0:T(8,128)S(1)}, u32[]{:S(2)}, u32[]{:S(2)}) collective-permute-start(f32[8,128]{1,0:T(8,128)S(1)} %copy-done.1), channel_id=1, source_target_pairs={{0,1},{1,0},{2,3},{3,2},{4,5},{5,4},{6,7},{7,6},{8,9},{9,8},{10,11... | collective-permute-start | bytes 12296 | tf_op jit(solution)/shard_map/ppermute | solution.py:190
  8.7 6.2 %collective-permute-start.6 = (f32[2,8,128]{2,1,0:T(8,128)S(1)}, f32[2,8,128]{2,1,0:T(8,128)S(1)}, u32[]{:S(2)}, u32[]{:S(2)}) collective-permute-start(f32[2,8,128]{2,1,0:T(8,128)S(1)} %shard_map.59.refs_0_), channel_id=1, source_target_pairs={{0,3},{1,2},{2,1},{3,0},{4,7},{5,6},{6,5},{7,4},{8,11},{9,10},{10,... | collective-permute-start | bytes 24584 | tf_op jit(solution)/shard_map/ppermute | solution.py:190
  10.0 6.5 %collective-permute-start.2 = (f32[4,8,128]{2,1,0:T(8,128)S(1)}, f32[4,8,128]{2,1,0:T(8,128)S(1)}, u32[]{:S(2)}, u32[]{:S(2)}) collective-permute-start(f32[4,8,128]{2,1,0:T(8,128)S(1)} %shard_map.56.refs_0_), channel_id=1, source_target_pairs={{0,16},{4,20},{8,24},{12,28},{16,0},{20,4},{24,8},{28,12},{1,17},{... | collective-permute-start | bytes 49160 | tf_op jit(solution)/shard_map/ppermute | solution.py:190
  15.2 3.7 %collective-permute-start.7 = (f32[4,8,128]{2,1,0:T(8,128)S(1)}, f32[4,8,128]{2,1,0:T(8,128)S(1)}, u32[]{:S(2)}, u32[]{:S(2)}) collective-permute-start(f32[4,8,128]{2,1,0:T(8,128)S(1)} %get-tuple-element.24), channel_id=1, source_target_pairs={{0,4},{4,0},{8,12},{12,8},{16,20},{20,16},{24,28},{28,24},{1,5},{5... | collective-permute-start | bytes 49160 | tf_op jit(solution)/shard_map/ppermute | solution.py:190
  17.1 6.3 %collective-permute-start.3 = (f32[2,8,128]{2,1,0:T(8,128)S(1)}, f32[2,8,128]{2,1,0:T(8,128)S(1)}, u32[]{:S(2)}, u32[]{:S(2)}) collective-permute-start(f32[2,8,128]{2,1,0:T(8,128)S(1)} %get-tuple-element.20), channel_id=1, source_target_pairs={{0,3},{1,2},{2,1},{3,0},{4,7},{5,6},{6,5},{7,4},{8,11},{9,10},{10,... | collective-permute-start | bytes 24584 | tf_op jit(solution)/shard_map/ppermute | solution.py:190
  19.0 5.4 %collective-permute-start.10 = (f32[1,8,128]{2,1,0:T(8,128)S(1)}, f32[1,8,128]{2,1,0:T(8,128)S(1)}, u32[]{:S(2)}, u32[]{:S(2)}) collective-permute-start(f32[1,8,128]{2,1,0:T(8,128)S(1)} %get-tuple-element.28), channel_id=1, source_target_pairs={{0,24},{4,28},{8,16},{12,20},{16,8},{20,12},{24,0},{28,4},{1,25},{... | collective-permute-start | bytes 12296 | tf_op jit(solution)/shard_map/ppermute | solution.py:190
  20.3 4.5 %collective-permute-start.9 = (f32[1,8,128]{2,1,0:T(8,128)S(1)}, f32[1,8,128]{2,1,0:T(8,128)S(1)}, u32[]{:S(2)}, u32[]{:S(2)}) collective-permute-start(f32[1,8,128]{2,1,0:T(8,128)S(1)} %get-tuple-element.27), channel_id=1, source_target_pairs={{0,16},{4,20},{8,24},{12,28},{16,0},{20,4},{24,8},{28,12},{1,17},{... | collective-permute-start | bytes 12296 | tf_op jit(solution)/shard_map/ppermute | solution.py:190
  22.0 3.6 %collective-permute-start.8 = (f32[1,8,128]{2,1,0:T(8,128)S(1)}, f32[1,8,128]{2,1,0:T(8,128)S(1)}, u32[]{:S(2)}, u32[]{:S(2)}) collective-permute-start(f32[1,8,128]{2,1,0:T(8,128)S(1)} %get-tuple-element.26), channel_id=1, source_target_pairs={{0,8},{4,12},{8,0},{12,4},{16,24},{20,28},{24,16},{28,20},{1,9},{5... | collective-permute-start | bytes 12296 | tf_op jit(solution)/shard_map/ppermute | solution.py:190
  23.4 2.3 %collective-permute-start.4 = (f32[1,8,128]{2,1,0:T(8,128)S(1)}, f32[1,8,128]{2,1,0:T(8,128)S(1)}, u32[]{:S(2)}, u32[]{:S(2)}) collective-permute-start(f32[1,8,128]{2,1,0:T(8,128)S(1)} %get-tuple-element.22), channel_id=1, source_target_pairs={{0,1},{1,0},{2,3},{3,2},{4,5},{5,4},{6,7},{7,6},{8,9},{9,8},{10,11... | collective-permute-start | bytes 12296 | tf_op jit(solution)/shard_map/ppermute | solution.py:190

commit v2 on v1

--- a/solution.py
+++ b/solution.py
@@ -52,13 +52,17 @@
     acc[...] = jnp.zeros_like(acc)
 
 
+def count_kernel(count, used):
+    used[...] = jnp.full(used.shape, count[0, 0], used.dtype)
+
+
 def build_kernel(blk, values, rows, cols, count, start, hi, lo, acc):
     del start
     r, c = lax.axis_index("row"), lax.axis_index("col")
     half = blk // 2
     steps = half // SUB
     group = half * SUB
-    used = jnp.broadcast_to(count[...], (SUB, LANES))
+    used = count[...]
     side = lax.broadcasted_iota(jnp.int32, (SUB, LANES), 1) // blk
 
     def add_slot(k, first):
@@ -96,6 +100,14 @@
         cost_estimate=pl.CostEstimate(flops=1 << 20, bytes_accessed=2 << 20, transcendentals=0),
         name="init",
     )()
+    used = pl.pallas_call(
+        count_kernel,
+        out_shape=jax.ShapeDtypeStruct((SUB, LANES), jnp.int32),
+        in_specs=[SMEM],
+        out_specs=VMEM,
+        compiler_params=pltpu.CompilerParams(vmem_limit_bytes=1 << 20),
+        name="count",
+    )(counts)
     hi, lo, _ = pl.pallas_call(
         functools.partial(build_kernel, blk),
         out_shape=[jax.ShapeDtypeStruct(shape, bf16)] * 2 + [jax.ShapeDtypeStruct(shape, f32)],
@@ -105,7 +117,7 @@
         compiler_params=pltpu.CompilerParams(vmem_limit_bytes=12 << 20),
         cost_estimate=pl.CostEstimate(flops=1 << 20, bytes_accessed=6 << 20, transcendentals=0),
         name="build",
-    )(view, block_rows, block_cols, counts, start)
+    )(view, block_rows, block_cols, used, start)
     return vectors, hi, lo
 
 

time: 26.4 us -> 26.4 us (level)
  no operation moved by 1% of the time
where the time goes in v2:
time: 26.4 us; the launch traced here: 26.2 us
  starting transfers between devices  14.5 us (55%)
  waiting for transfers between devices  7.12 us (27%)
  Pallas kernels  2.64 us (10%)
  between operations  0.72 us (3%)
  local copies, waits for them, and re-layouts  0.7 us (3%)
  other arithmetic  0.6 us (2%)
    ppermute x11, starting transfers between devices, trade(): return lax.ppermute(x, axis, [(i, i ^ step) for i in range(n)])  14.5 us
    ppermute x11, waiting for transfers between devices, trade(): return lax.ppermute(x, axis, [(i, i ^ step) for i in range(n)])  7.12 us
    pallas_call x1, Pallas kernels, build(): pl.pallas_call(functools.partial(build_kernel, blk), out_shape=[jax.Shape...  1.47 us
    pallas_call x2, Pallas kernels, call(): pl.pallas_call(functools.partial(kernel, len(xs), take, put), out_shape=[...  1.02 us
    unnamed x8, local copies, waits for them, and re-layouts  0.7 us
    squeeze x1, other arithmetic, exchange(): return (g0 + last + w)[0]  0.6 us
  transfers between devices with their start and end apart: 11, of which 6 were waited for; matrix products, arithmetic and copies ran while one was open for 0% of the time, Pallas kernels for 10%

profile of v2, /device:TPU:0, one launch (start us, length us, event | category | flops | bytes accessed | tf_op | source)
XLA Modules:
  0.0 26.2 jit_solution(5744353458432600594)
XLA Ops:
  0.0 0.0 copy-start
  0.0 3.1 %collective-permute-start = (f32[8,128]{1,0:T(8,128)}, f32[8,128]{1,0:T(8,128)S(1)}, u32[]{:S(2)}, u32[]{:S(2)}) collective-permute-start(f32[8,128]{1,0:T(8,128)} %refs_0_.3), channel_id=1, source_target_pairs={{0,8},{4,12},{8,0},{12,4},{16,24},{20,28},{24,16},{28,20},{1,9},{5... | collective-permute-start | bytes 12296 | tf_op jit(solution)/shard_map/ppermute | solution.py:202
  3.1 1.8 %collective-permute-done.refs_1_ = f32[8,128]{1,0:T(8,128)S(1)} collective-permute-done((f32[8,128]{1,0:T(8,128)}, f32[8,128]{1,0:T(8,128)S(1)}, u32[]{:S(2)}, u32[]{:S(2)}) %collective-permute-start) | collective-permute-done | bytes 4128 | tf_op jit(solution)/shard_map/ppermute | solution.py:202
  4.8 0.0 copy-start.1
  4.9 0.7 %copy-done.1 = f32[8,128]{1,0:T(8,128)S(1)} copy-done((f32[8,128]{1,0:T(8,128)S(1)}, f32[8,128]{1,0:T(8,128)}, u32[]{:S(2)}) %copy-start.1) | copy-done | bytes 4120
  5.5 0.0 copy-start.2
  5.5 0.0 copy-start.3
  5.5 1.9 %collective-permute-start.1 = (f32[2,8,128]{2,1,0:T(8,128)S(1)}, f32[2,8,128]{2,1,0:T(8,128)S(1)}, u32[]{:S(2)}, u32[]{:S(2)}) collective-permute-start(f32[2,8,128]{2,1,0:T(8,128)S(1)} %shard_map.55.refs_0_), channel_id=1, source_target_pairs={{0,4},{4,0},{8,12},{12,8},{16,20},{20,16},{24,28},{28,24},{1,5},{5... | collective-permute-start | bytes 24584 | tf_op jit(solution)/shard_map/ppermute | solution.py:202
  7.5 0.0 collective-permute-start.5
  7.5 1.2 %collective-permute-done.5.refs_1_ = f32[8,128]{1,0:T(8,128)S(1)} collective-permute-done((f32[8,128]{1,0:T(8,128)S(1)}, f32[8,128]{1,0:T(8,128)S(1)}, u32[]{:S(2)}, u32[]{:S(2)}) %collective-permute-start.5) | collective-permute-done | bytes 4128 | tf_op jit(solution)/shard_map/ppermute | solution.py:202
  8.7 1.3 %collective-permute-start.6 = (f32[2,8,128]{2,1,0:T(8,128)S(1)}, f32[2,8,128]{2,1,0:T(8,128)S(1)}, u32[]{:S(2)}, u32[]{:S(2)}) collective-permute-start(f32[2,8,128]{2,1,0:T(8,128)S(1)} %shard_map.59.refs_0_), channel_id=1, source_target_pairs={{0,3},{1,2},{2,1},{3,0},{4,7},{5,6},{6,5},{7,4},{8,11},{9,10},{10,... | collective-permute-start | bytes 24584 | tf_op jit(solution)/shard_map/ppermute | solution.py:202
  9.9 0.0 collective-permute-done.1.refs_1_
  10.0 2.6 %collective-permute-start.2 = (f32[4,8,128]{2,1,0:T(8,128)S(1)}, f32[4,8,128]{2,1,0:T(8,128)S(1)}, u32[]{:S(2)}, u32[]{:S(2)}) collective-permute-start(f32[4,8,128]{2,1,0:T(8,128)S(1)} %shard_map.56.refs_0_), channel_id=1, source_target_pairs={{0,16},{4,20},{8,24},{12,28},{16,0},{20,4},{24,8},{28,12},{1,17},{... | collective-permute-start | bytes 49160 | tf_op jit(solution)/shard_map/ppermute | solution.py:202
  13.2 0.1 init.1.start
  13.3 0.0 copy-done
  13.4 0.0 copy-done.2
  13.4 0.0 copy-done.3
  13.4 1.5 %build.1 = (bf16[8,512,128]{2,1,0:T(8,128)(2,1)S(1)}, bf16[8,512,128]{2,1,0:T(8,128)(2,1)S(1)}, f32[8,512,128]{2,1,0:T(8,128)S(1)}) custom-call(f32[2048,128]{1,0:T(8,128)S(1)} %bitcast.7, s32[1,64]{1,0:T(1,128)S(1)} %copy-done.2, s32[1,64]{1,0:T(1,128)S(1)} %copy-done.3, s32[8,128]{1,0:T(8,128)S(1)} %count.2, ...), custom_call_target="tpu_custom_call", output_to_operand_aliasing={{2}: (4, {})} | custom-call | flops 1048576 | bytes 6291456 | tf_op jit(solution)/shard_map/build/pallas_call | solution.py:111
  14.8 0.0 collective-permute-done.6.refs_1_
  14.9 0.4 %shard_map.60 = (f32[4,8,128]{2,1,0:T(8,128)S(1)}, f32[4,8,128]{2,1,0:T(8,128)S(1)}) custom-call(f32[2,8,128]{2,1,0:T(8,128)S(1)} %shard_map.59.refs_0_, f32[2,8,128]{2,1,0:T(8,128)S(1)} %collective-permute-done.6.refs_1_, bf16[8,512,128]{2,1,0:T(8,128)(2,1)S(1)} %get-tuple-element.17.refs_2_, bf16[8,512,128]{2,1,0:T(8,128)(2,1)S(1)} %get-tuple-element.18.refs_3_), custom_call_target="tpu_custom_call" | custom-call | flops 67108864 | bytes 2097152 | tf_op jit(solution)/shard_map/pallas_call | solution.py:182
  15.2 1.2 %collective-permute-start.7 = (f32[4,8,128]{2,1,0:T(8,128)S(1)}, f32[4,8,128]{2,1,0:T(8,128)S(1)}, u32[]{:S(2)}, u32[]{:S(2)}) collective-permute-start(f32[4,8,128]{2,1,0:T(8,128)S(1)} %get-tuple-element.24), channel_id=1, source_target_pairs={{0,4},{4,0},{8,12},{12,8},{16,20},{20,16},{24,28},{28,24},{1,5},{5... | collective-permute-start | bytes 49160 | tf_op jit(solution)/shard_map/ppermute | solution.py:202
  16.4 0.0 collective-permute-done.2.refs_1_
  16.4 0.6 %shard_map.57 = (f32[2,8,128]{2,1,0:T(8,128)S(1)}, f32[2,8,128]{2,1,0:T(8,128)S(1)}) custom-call(f32[4,8,128]{2,1,0:T(8,128)S(1)} %shard_map.56.refs_0_, f32[4,8,128]{2,1,0:T(8,128)S(1)} %collective-permute-done.2.refs_1_, bf16[8,512,128]{2,1,0:T(8,128)(2,1)S(1)} %get-tuple-element.17.refs_2_, bf16[8,512,128]{2,1,0:T(8,128)(2,1)S(1)} %get-tuple-element.18.refs_3_), custom_call_target="tpu_custom_call" | custom-call | flops 67108864 | bytes 2097152 | tf_op jit(solution)/shard_map/pallas_call | solution.py:182
  17.1 0.0 collective-permute-start.3
  17.1 1.9 %collective-permute-done.7.b = f32[4,8,128]{2,1,0:T(8,128)S(1)} collective-permute-done((f32[4,8,128]{2,1,0:T(8,128)S(1)}, f32[4,8,128]{2,1,0:T(8,128)S(1)}, u32[]{:S(2)}, u32[]{:S(2)}) %collective-permute-start.7) | collective-permute-done | bytes 16416 | tf_op jit(solution)/shard_map/ppermute | solution.py:202
  19.0 1.3 %collective-permute-start.10 = (f32[1,8,128]{2,1,0:T(8,128)S(1)}, f32[1,8,128]{2,1,0:T(8,128)S(1)}, u32[]{:S(2)}, u32[]{:S(2)}) collective-permute-start(f32[1,8,128]{2,1,0:T(8,128)S(1)} %get-tuple-element.28), channel_id=1, source_target_pairs={{0,24},{4,28},{8,16},{12,20},{16,8},{20,12},{24,0},{28,4},{1,25},{... | collective-permute-start | bytes 12296 | tf_op jit(solution)/shard_map/ppermute | solution.py:202
  20.3 1.7 %collective-permute-start.9 = (f32[1,8,128]{2,1,0:T(8,128)S(1)}, f32[1,8,128]{2,1,0:T(8,128)S(1)}, u32[]{:S(2)}, u32[]{:S(2)}) collective-permute-start(f32[1,8,128]{2,1,0:T(8,128)S(1)} %get-tuple-element.27), channel_id=1, source_target_pairs={{0,16},{4,20},{8,24},{12,28},{16,0},{20,4},{24,8},{28,12},{1,17},{... | collective-permute-start | bytes 12296 | tf_op jit(solution)/shard_map/ppermute | solution.py:202
  22.0 1.3 %collective-permute-start.8 = (f32[1,8,128]{2,1,0:T(8,128)S(1)}, f32[1,8,128]{2,1,0:T(8,128)S(1)}, u32[]{:S(2)}, u32[]{:S(2)}) collective-permute-start(f32[1,8,128]{2,1,0:T(8,128)S(1)} %get-tuple-element.26), channel_id=1, source_target_pairs={{0,8},{4,12},{8,0},{12,4},{16,24},{20,28},{24,16},{28,20},{1,9},{5... | collective-permute-start | bytes 12296 | tf_op jit(solution)/shard_map/ppermute | solution.py:202
  23.4 0.0 collective-permute-done.3.b
  23.4 0.0 collective-permute-start.4
  23.4 1.0 %collective-permute-done.10 = f32[1,8,128]{2,1,0:T(8,128)S(1)} collective-permute-done((f32[1,8,128]{2,1,0:T(8,128)S(1)}, f32[1,8,128]{2,1,0:T(8,128)S(1)}, u32[]{:S(2)}, u32[]{:S(2)}) %collective-permute-start.10) | collective-permute-done | bytes 4128 | tf_op jit(solution)/shard_map/ppermute | solution.py:202
  24.4 0.4 %collective-permute-done.9 = f32[1,8,128]{2,1,0:T(8,128)S(1)} collective-permute-done((f32[1,8,128]{2,1,0:T(8,128)S(1)}, f32[1,8,128]{2,1,0:T(8,128)S(1)}, u32[]{:S(2)}, u32[]{:S(2)}) %collective-permute-start.9) | collective-permute-done | bytes 4128 | tf_op jit(solution)/shard_map/ppermute | solution.py:202
  24.9 0.8 %collective-permute-done.8 = f32[1,8,128]{2,1,0:T(8,128)S(1)} collective-permute-done((f32[1,8,128]{2,1,0:T(8,128)S(1)}, f32[1,8,128]{2,1,0:T(8,128)S(1)}, u32[]{:S(2)}, u32[]{:S(2)}) %collective-permute-start.8) | collective-permute-done | bytes 4128 | tf_op jit(solution)/shard_map/ppermute | solution.py:202
  25.6 0.0 collective-permute-done.4
  25.6 0.6 %add_bitcast_fusion = f32[8,128]{1,0:T(8,128)} fusion(f32[1,8,128]{2,1,0:T(8,128)S(1)} %collective-permute-done.10, f32[1,8,128]{2,1,0:T(8,128)S(1)} %collective-permute-done.9, f32[1,8,128]{2,1,0:T(8,128)S(1)} %get-tuple-element.25, f32[1,8,128]{2,1,0:T(8,128)S(1)} %collective-permute-done.8, f32[1,8,128]{2,1,0:T(8,128)S(1)} %get-tuple-element.21, ...), kind=kLoop, calls=%fused_computation | loop fusion | flops 5120 | bytes 28672 | tf_op jit(solution)/shard_map/squeeze | solution.py:250
  (6 shorter events, 0.0 us)
Async XLA Ops:
  0.0 13.3 %copy-start = (f32[64,4096]{1,0:T(8,128)S(1)}, f32[64,4096]{1,0:T(8,128)}, u32[]{:S(2)}) copy-start(f32[64,4096]{1,0:T(8,128)} %param.6) | copy-start | bytes 3145732
  0.0 4.8 %collective-permute-start = (f32[8,128]{1,0:T(8,128)}, f32[8,128]{1,0:T(8,128)S(1)}, u32[]{:S(2)}, u32[]{:S(2)}) collective-permute-start(f32[8,128]{1,0:T(8,128)} %refs_0_.3), channel_id=1, source_target_pairs={{0,8},{4,12},{8,0},{12,4},{16,24},{20,28},{24,16},{28,20},{1,9},{5... | collective-permute-start | bytes 12296 | tf_op jit(solution)/shard_map/ppermute | solution.py:202
  4.8 0.7 %copy-start.1 = (f32[8,128]{1,0:T(8,128)S(1)}, f32[8,128]{1,0:T(8,128)}, u32[]{:S(2)}) copy-start(f32[8,128]{1,0:T(8,128)} %refs_0_.3) | copy-start | bytes 12292
  5.5 7.8 %copy-start.2 = (s32[1,64]{1,0:T(1,128)S(1)}, s32[1,64]{1,0:T(1,128)}, u32[]{:S(2)}) copy-start(s32[1,64]{1,0:T(1,128)} %rows.1) | copy-start | bytes 772
  5.5 7.8 %copy-start.3 = (s32[1,64]{1,0:T(1,128)S(1)}, s32[1,64]{1,0:T(1,128)}, u32[]{:S(2)}) copy-start(s32[1,64]{1,0:T(1,128)} %cols.1) | copy-start | bytes 772
  5.5 4.4 %collective-permute-start.1 = (f32[2,8,128]{2,1,0:T(8,128)S(1)}, f32[2,8,128]{2,1,0:T(8,128)S(1)}, u32[]{:S(2)}, u32[]{:S(2)}) collective-permute-start(f32[2,8,128]{2,1,0:T(8,128)S(1)} %shard_map.55.refs_0_), channel_id=1, source_target_pairs={{0,4},{4,0},{8,12},{12,8},{16,20},{20,16},{24,28},{28,24},{1,5},{5... | collective-permute-start | bytes 24584 | tf_op jit(solution)/shard_map/ppermute | solution.py:202
  7.5 1.2 %collective-permute-start.5 = (f32[8,128]{1,0:T(8,128)S(1)}, f32[8,128]{1,0:T(8,128)S(1)}, u32[]{:S(2)}, u32[]{:S(2)}) collective-permute-start(f32[8,128]{1,0:T(8,128)S(1)} %copy-done.1), channel_id=1, source_target_pairs={{0,1},{1,0},{2,3},{3,2},{4,5},{5,4},{6,7},{7,6},{8,9},{9,8},{10,11... | collective-permute-start | bytes 12296 | tf_op jit(solution)/shard_map/ppermute | solution.py:202
  8.7 6.2 %collective-permute-start.6 = (f32[2,8,128]{2,1,0:T(8,128)S(1)}, f32[2,8,128]{2,1,0:T(8,128)S(1)}, u32[]{:S(2)}, u32[]{:S(2)}) collective-permute-start(f32[2,8,128]{2,1,0:T(8,128)S(1)} %shard_map.59.refs_0_), channel_id=1, source_target_pairs={{0,3},{1,2},{2,1},{3,0},{4,7},{5,6},{6,5},{7,4},{8,11},{9,10},{10,... | collective-permute-start | bytes 24584 | tf_op jit(solution)/shard_map/ppermute | solution.py:202
  10.0 6.5 %collective-permute-start.2 = (f32[4,8,128]{2,1,0:T(8,128)S(1)}, f32[4,8,128]{2,1,0:T(8,128)S(1)}, u32[]{:S(2)}, u32[]{:S(2)}) collective-permute-start(f32[4,8,128]{2,1,0:T(8,128)S(1)} %shard_map.56.refs_0_), channel_id=1, source_target_pairs={{0,16},{4,20},{8,24},{12,28},{16,0},{20,4},{24,8},{28,12},{1,17},{... | collective-permute-start | bytes 49160 | tf_op jit(solution)/shard_map/ppermute | solution.py:202
  15.2 3.7 %collective-permute-start.7 = (f32[4,8,128]{2,1,0:T(8,128)S(1)}, f32[4,8,128]{2,1,0:T(8,128)S(1)}, u32[]{:S(2)}, u32[]{:S(2)}) collective-permute-start(f32[4,8,128]{2,1,0:T(8,128)S(1)} %get-tuple-element.24), channel_id=1, source_target_pairs={{0,4},{4,0},{8,12},{12,8},{16,20},{20,16},{24,28},{28,24},{1,5},{5... | collective-permute-start | bytes 49160 | tf_op jit(solution)/shard_map/ppermute | solution.py:202
  17.1 6.3 %collective-permute-start.3 = (f32[2,8,128]{2,1,0:T(8,128)S(1)}, f32[2,8,128]{2,1,0:T(8,128)S(1)}, u32[]{:S(2)}, u32[]{:S(2)}) collective-permute-start(f32[2,8,128]{2,1,0:T(8,128)S(1)} %get-tuple-element.20), channel_id=1, source_target_pairs={{0,3},{1,2},{2,1},{3,0},{4,7},{5,6},{6,5},{7,4},{8,11},{9,10},{10,... | collective-permute-start | bytes 24584 | tf_op jit(solution)/shard_map/ppermute | solution.py:202
  19.0 5.4 %collective-permute-start.10 = (f32[1,8,128]{2,1,0:T(8,128)S(1)}, f32[1,8,128]{2,1,0:T(8,128)S(1)}, u32[]{:S(2)}, u32[]{:S(2)}) collective-permute-start(f32[1,8,128]{2,1,0:T(8,128)S(1)} %get-tuple-element.28), channel_id=1, source_target_pairs={{0,24},{4,28},{8,16},{12,20},{16,8},{20,12},{24,0},{28,4},{1,25},{... | collective-permute-start | bytes 12296 | tf_op jit(solution)/shard_map/ppermute | solution.py:202
  20.3 4.5 %collective-permute-start.9 = (f32[1,8,128]{2,1,0:T(8,128)S(1)}, f32[1,8,128]{2,1,0:T(8,128)S(1)}, u32[]{:S(2)}, u32[]{:S(2)}) collective-permute-start(f32[1,8,128]{2,1,0:T(8,128)S(1)} %get-tuple-element.27), channel_id=1, source_target_pairs={{0,16},{4,20},{8,24},{12,28},{16,0},{20,4},{24,8},{28,12},{1,17},{... | collective-permute-start | bytes 12296 | tf_op jit(solution)/shard_map/ppermute | solution.py:202
  22.0 3.6 %collective-permute-start.8 = (f32[1,8,128]{2,1,0:T(8,128)S(1)}, f32[1,8,128]{2,1,0:T(8,128)S(1)}, u32[]{:S(2)}, u32[]{:S(2)}) collective-permute-start(f32[1,8,128]{2,1,0:T(8,128)S(1)} %get-tuple-element.26), channel_id=1, source_target_pairs={{0,8},{4,12},{8,0},{12,4},{16,24},{20,28},{24,16},{28,20},{1,9},{5... | collective-permute-start | bytes 12296 | tf_op jit(solution)/shard_map/ppermute | solution.py:202
  23.4 2.3 %collective-permute-start.4 = (f32[1,8,128]{2,1,0:T(8,128)S(1)}, f32[1,8,128]{2,1,0:T(8,128)S(1)}, u32[]{:S(2)}, u32[]{:S(2)}) collective-permute-start(f32[1,8,128]{2,1,0:T(8,128)S(1)} %get-tuple-element.22), channel_id=1, source_target_pairs={{0,1},{1,0},{2,3},{3,2},{4,5},{5,4},{6,7},{7,6},{8,9},{9,8},{10,11... | collective-permute-start | bytes 12296 | tf_op jit(solution)/shard_map/ppermute | solution.py:202

commit v3 on v2

--- a/solution.py
+++ b/solution.py
@@ -63,18 +63,19 @@
     steps = half // SUB
     group = half * SUB
     used = count[...]
+    span = 2 * (acc.shape[1] // blk)
+    codes = (cols[...] ^ (r * 2)) * (span // 2) + (rows[...] ^ (c * 2))
     side = lax.broadcasted_iota(jnp.int32, (SUB, LANES), 1) // blk
 
     def add_slot(k, first):
-        br = rows[0, k] ^ (c * 2)
-        bc = cols[0, k] ^ (r * 2)
-        q, odd = bc // 2, bc % 2
+        code = codes[0, k]
+        q, odd, base = code // span, code // (span // 2) % 2, code % (span // 2) * blk
         keep = (side == odd) & (used > k)
         swapped = jnp.broadcast_to(odd, (SUB, LANES)) == 1
         for s in range(steps):
             two = values[pl.ds(first + s * SUB * SUB, SUB, stride=SUB), :]
             turn = swap(two)
-            at = br * blk + 2 * SUB * s
+            at = base + 2 * SUB * s
             acc[q, pl.ds(at, SUB, stride=2), :] += jnp.where(keep, jnp.where(swapped, turn, two), 0.0)
             acc[q, pl.ds(at + 1, SUB, stride=2), :] += jnp.where(keep, jnp.where(swapped, two, turn), 0.0)
 
@@ -111,7 +112,7 @@
     hi, lo, _ = pl.pallas_call(
         functools.partial(build_kernel, blk),
         out_shape=[jax.ShapeDtypeStruct(shape, bf16)] * 2 + [jax.ShapeDtypeStruct(shape, f32)],
-        in_specs=[VMEM, SMEM, SMEM, VMEM, VMEM],
+        in_specs=[VMEM] * 5,
         out_specs=[VMEM] * 3,
         input_output_aliases={4: 2},
         compiler_params=pltpu.CompilerParams(vmem_limit_bytes=12 << 20),

time: 26.4 us -> 26.1 us (0.989)
  Pallas kernels: 2.64 us -> 2.36 us
    pallas_call x1, Pallas kernels: 1.47 us -> 1.18 us  [build(): pl.pallas_call(functools.partial(build_kernel, blk), out_shape=[jax.Shape...]
  transfers between devices with their start and end apart: 11 -> 11, of which waited for: 6 -> 6; matrix products, arithmetic and copies ran while one was open for 0% -> 0% of each run, Pallas kernels for 10% -> 9%
where the time goes in v3:
time: 26.1 us; the launch traced here: 26 us
  starting transfers between devices  14.5 us (56%)
  waiting for transfers between devices  7.12 us (27%)
  Pallas kernels  2.36 us (9%)
  between operations  0.72 us (3%)
  local copies, waits for them, and re-layouts  0.7 us (3%)
  other arithmetic  0.6 us (2%)
    ppermute x11, starting transfers between devices, trade(): return lax.ppermute(x, axis, [(i, i ^ step) for i in range(n)])  14.5 us
    ppermute x11, waiting for transfers between devices, trade(): return lax.ppermute(x, axis, [(i, i ^ step) for i in range(n)])  7.12 us
    pallas_call x1, Pallas kernels, build(): pl.pallas_call(functools.partial(build_kernel, blk), out_shape=[jax.Shape...  1.18 us
    pallas_call x2, Pallas kernels, call(): pl.pallas_call(functools.partial(kernel, len(xs), take, put), out_shape=[...  1.02 us
    unnamed x8, local copies, waits for them, and re-layouts  0.7 us
    squeeze x1, other arithmetic, exchange(): return (g0 + last + w)[0]  0.6 us
  transfers between devices with their start and end apart: 11, of which 6 were waited for; matrix products, arithmetic and copies ran while one was open for 0% of the time, Pallas kernels for 9%

profile of v3, /device:TPU:0, one launch (start us, length us, event | category | flops | bytes accessed | tf_op | source)
XLA Modules:
  0.0 26.0 jit_solution(9536899366192370020)
XLA Ops:
  0.0 0.0 copy-start
  0.0 3.1 %collective-permute-start = (f32[8,128]{1,0:T(8,128)}, f32[8,128]{1,0:T(8,128)S(1)}, u32[]{:S(2)}, u32[]{:S(2)}) collective-permute-start(f32[8,128]{1,0:T(8,128)} %refs_0_.3), channel_id=1, source_target_pairs={{0,8},{4,12},{8,0},{12,4},{16,24},{20,28},{24,16},{28,20},{1,9},{5... | collective-permute-start | bytes 12296 | tf_op jit(solution)/shard_map/ppermute | solution.py:203
  3.1 1.8 %collective-permute-done.refs_1_ = f32[8,128]{1,0:T(8,128)S(1)} collective-permute-done((f32[8,128]{1,0:T(8,128)}, f32[8,128]{1,0:T(8,128)S(1)}, u32[]{:S(2)}, u32[]{:S(2)}) %collective-permute-start) | collective-permute-done | bytes 4128 | tf_op jit(solution)/shard_map/ppermute | solution.py:203
  4.8 0.0 copy-start.1
  4.9 0.7 %copy-done.1 = f32[8,128]{1,0:T(8,128)S(1)} copy-done((f32[8,128]{1,0:T(8,128)S(1)}, f32[8,128]{1,0:T(8,128)}, u32[]{:S(2)}) %copy-start.1) | copy-done | bytes 4120
  5.5 0.0 copy-start.2
  5.5 0.0 copy-start.3
  5.5 1.9 %collective-permute-start.1 = (f32[2,8,128]{2,1,0:T(8,128)S(1)}, f32[2,8,128]{2,1,0:T(8,128)S(1)}, u32[]{:S(2)}, u32[]{:S(2)}) collective-permute-start(f32[2,8,128]{2,1,0:T(8,128)S(1)} %shard_map.55.refs_0_), channel_id=1, source_target_pairs={{0,4},{4,0},{8,12},{12,8},{16,20},{20,16},{24,28},{28,24},{1,5},{5... | collective-permute-start | bytes 24584 | tf_op jit(solution)/shard_map/ppermute | solution.py:203
  7.5 0.0 collective-permute-start.5
  7.5 1.2 %collective-permute-done.5.refs_1_ = f32[8,128]{1,0:T(8,128)S(1)} collective-permute-done((f32[8,128]{1,0:T(8,128)S(1)}, f32[8,128]{1,0:T(8,128)S(1)}, u32[]{:S(2)}, u32[]{:S(2)}) %collective-permute-start.5) | collective-permute-done | bytes 4128 | tf_op jit(solution)/shard_map/ppermute | solution.py:203
  8.7 1.3 %collective-permute-start.6 = (f32[2,8,128]{2,1,0:T(8,128)S(1)}, f32[2,8,128]{2,1,0:T(8,128)S(1)}, u32[]{:S(2)}, u32[]{:S(2)}) collective-permute-start(f32[2,8,128]{2,1,0:T(8,128)S(1)} %shard_map.59.refs_0_), channel_id=1, source_target_pairs={{0,3},{1,2},{2,1},{3,0},{4,7},{5,6},{6,5},{7,4},{8,11},{9,10},{10,... | collective-permute-start | bytes 24584 | tf_op jit(solution)/shard_map/ppermute | solution.py:203
  9.9 0.0 collective-permute-done.1.refs_1_
  10.0 2.6 %collective-permute-start.2 = (f32[4,8,128]{2,1,0:T(8,128)S(1)}, f32[4,8,128]{2,1,0:T(8,128)S(1)}, u32[]{:S(2)}, u32[]{:S(2)}) collective-permute-start(f32[4,8,128]{2,1,0:T(8,128)S(1)} %shard_map.56.refs_0_), channel_id=1, source_target_pairs={{0,16},{4,20},{8,24},{12,28},{16,0},{20,4},{24,8},{28,12},{1,17},{... | collective-permute-start | bytes 49160 | tf_op jit(solution)/shard_map/ppermute | solution.py:203
  13.2 0.1 init.1.start
  13.3 0.0 copy-done
  13.4 0.0 copy-done.2
  13.4 0.0 copy-done.3
  13.4 1.2 %build.1 = (bf16[8,512,128]{2,1,0:T(8,128)(2,1)S(1)}, bf16[8,512,128]{2,1,0:T(8,128)(2,1)S(1)}, f32[8,512,128]{2,1,0:T(8,128)S(1)}) custom-call(f32[2048,128]{1,0:T(8,128)S(1)} %bitcast.7, s32[1,64]{1,0:T(1,128)S(1)} %copy-done.2, s32[1,64]{1,0:T(1,128)S(1)} %copy-done.3, s32[8,128]{1,0:T(8,128)S(1)} %count.2, ...), custom_call_target="tpu_custom_call", output_to_operand_aliasing={{2}: (4, {})} | custom-call | flops 1048576 | bytes 6291456 | tf_op jit(solution)/shard_map/build/pallas_call | solution.py:112
  14.6 0.0 collective-permute-done.6.refs_1_
  14.6 0.4 %shard_map.60 = (f32[4,8,128]{2,1,0:T(8,128)S(1)}, f32[4,8,128]{2,1,0:T(8,128)S(1)}) custom-call(f32[2,8,128]{2,1,0:T(8,128)S(1)} %shard_map.59.refs_0_, f32[2,8,128]{2,1,0:T(8,128)S(1)} %collective-permute-done.6.refs_1_, bf16[8,512,128]{2,1,0:T(8,128)(2,1)S(1)} %get-tuple-element.17.refs_2_, bf16[8,512,128]{2,1,0:T(8,128)(2,1)S(1)} %get-tuple-element.18.refs_3_), custom_call_target="tpu_custom_call" | custom-call | flops 67108864 | bytes 2097152 | tf_op jit(solution)/shard_map/pallas_call | solution.py:183
  15.0 1.2 %collective-permute-start.7 = (f32[4,8,128]{2,1,0:T(8,128)S(1)}, f32[4,8,128]{2,1,0:T(8,128)S(1)}, u32[]{:S(2)}, u32[]{:S(2)}) collective-permute-start(f32[4,8,128]{2,1,0:T(8,128)S(1)} %get-tuple-element.24), channel_id=1, source_target_pairs={{0,4},{4,0},{8,12},{12,8},{16,20},{20,16},{24,28},{28,24},{1,5},{5... | collective-permute-start | bytes 49160 | tf_op jit(solution)/shard_map/ppermute | solution.py:203
  16.2 0.0 collective-permute-done.2.refs_1_
  16.2 0.6 %shard_map.57 = (f32[2,8,128]{2,1,0:T(8,128)S(1)}, f32[2,8,128]{2,1,0:T(8,128)S(1)}) custom-call(f32[4,8,128]{2,1,0:T(8,128)S(1)} %shard_map.56.refs_0_, f32[4,8,128]{2,1,0:T(8,128)S(1)} %collective-permute-done.2.refs_1_, bf16[8,512,128]{2,1,0:T(8,128)(2,1)S(1)} %get-tuple-element.17.refs_2_, bf16[8,512,128]{2,1,0:T(8,128)(2,1)S(1)} %get-tuple-element.18.refs_3_), custom_call_target="tpu_custom_call" | custom-call | flops 67108864 | bytes 2097152 | tf_op jit(solution)/shard_map/pallas_call | solution.py:183
  16.8 0.0 collective-permute-start.3
  16.8 1.9 %collective-permute-done.7.b = f32[4,8,128]{2,1,0:T(8,128)S(1)} collective-permute-done((f32[4,8,128]{2,1,0:T(8,128)S(1)}, f32[4,8,128]{2,1,0:T(8,128)S(1)}, u32[]{:S(2)}, u32[]{:S(2)}) %collective-permute-start.7) | collective-permute-done | bytes 16416 | tf_op jit(solution)/shard_map/ppermute | solution.py:203
  18.7 1.3 %collective-permute-start.10 = (f32[1,8,128]{2,1,0:T(8,128)S(1)}, f32[1,8,128]{2,1,0:T(8,128)S(1)}, u32[]{:S(2)}, u32[]{:S(2)}) collective-permute-start(f32[1,8,128]{2,1,0:T(8,128)S(1)} %get-tuple-element.28), channel_id=1, source_target_pairs={{0,24},{4,28},{8,16},{12,20},{16,8},{20,12},{24,0},{28,4},{1,25},{... | collective-permute-start | bytes 12296 | tf_op jit(solution)/shard_map/ppermute | solution.py:203
  20.1 1.7 %collective-permute-start.9 = (f32[1,8,128]{2,1,0:T(8,128)S(1)}, f32[1,8,128]{2,1,0:T(8,128)S(1)}, u32[]{:S(2)}, u32[]{:S(2)}) collective-permute-start(f32[1,8,128]{2,1,0:T(8,128)S(1)} %get-tuple-element.27), channel_id=1, source_target_pairs={{0,16},{4,20},{8,24},{12,28},{16,0},{20,4},{24,8},{28,12},{1,17},{... | collective-permute-start | bytes 12296 | tf_op jit(solution)/shard_map/ppermute | solution.py:203
  21.7 1.3 %collective-permute-start.8 = (f32[1,8,128]{2,1,0:T(8,128)S(1)}, f32[1,8,128]{2,1,0:T(8,128)S(1)}, u32[]{:S(2)}, u32[]{:S(2)}) collective-permute-start(f32[1,8,128]{2,1,0:T(8,128)S(1)} %get-tuple-element.26), channel_id=1, source_target_pairs={{0,8},{4,12},{8,0},{12,4},{16,24},{20,28},{24,16},{28,20},{1,9},{5... | collective-permute-start | bytes 12296 | tf_op jit(solution)/shard_map/ppermute | solution.py:203
  23.1 0.0 collective-permute-done.3.b
  23.1 0.0 collective-permute-start.4
  23.1 1.0 %collective-permute-done.10 = f32[1,8,128]{2,1,0:T(8,128)S(1)} collective-permute-done((f32[1,8,128]{2,1,0:T(8,128)S(1)}, f32[1,8,128]{2,1,0:T(8,128)S(1)}, u32[]{:S(2)}, u32[]{:S(2)}) %collective-permute-start.10) | collective-permute-done | bytes 4128 | tf_op jit(solution)/shard_map/ppermute | solution.py:203
  24.1 0.4 %collective-permute-done.9 = f32[1,8,128]{2,1,0:T(8,128)S(1)} collective-permute-done((f32[1,8,128]{2,1,0:T(8,128)S(1)}, f32[1,8,128]{2,1,0:T(8,128)S(1)}, u32[]{:S(2)}, u32[]{:S(2)}) %collective-permute-start.9) | collective-permute-done | bytes 4128 | tf_op jit(solution)/shard_map/ppermute | solution.py:203
  24.6 0.8 %collective-permute-done.8 = f32[1,8,128]{2,1,0:T(8,128)S(1)} collective-permute-done((f32[1,8,128]{2,1,0:T(8,128)S(1)}, f32[1,8,128]{2,1,0:T(8,128)S(1)}, u32[]{:S(2)}, u32[]{:S(2)}) %collective-permute-start.8) | collective-permute-done | bytes 4128 | tf_op jit(solution)/shard_map/ppermute | solution.py:203
  25.4 0.0 collective-permute-done.4
  25.4 0.6 %add_bitcast_fusion = f32[8,128]{1,0:T(8,128)} fusion(f32[1,8,128]{2,1,0:T(8,128)S(1)} %collective-permute-done.10, f32[1,8,128]{2,1,0:T(8,128)S(1)} %collective-permute-done.9, f32[1,8,128]{2,1,0:T(8,128)S(1)} %get-tuple-element.25, f32[1,8,128]{2,1,0:T(8,128)S(1)} %collective-permute-done.8, f32[1,8,128]{2,1,0:T(8,128)S(1)} %get-tuple-element.21, ...), kind=kLoop, calls=%fused_computation | loop fusion | flops 5120 | bytes 28672 | tf_op jit(solution)/shard_map/squeeze | solution.py:251
  (6 shorter events, 0.0 us)
Async XLA Ops:
  0.0 13.3 %copy-start = (f32[64,4096]{1,0:T(8,128)S(1)}, f32[64,4096]{1,0:T(8,128)}, u32[]{:S(2)}) copy-start(f32[64,4096]{1,0:T(8,128)} %param.6) | copy-start | bytes 3145732
  0.0 4.8 %collective-permute-start = (f32[8,128]{1,0:T(8,128)}, f32[8,128]{1,0:T(8,128)S(1)}, u32[]{:S(2)}, u32[]{:S(2)}) collective-permute-start(f32[8,128]{1,0:T(8,128)} %refs_0_.3), channel_id=1, source_target_pairs={{0,8},{4,12},{8,0},{12,4},{16,24},{20,28},{24,16},{28,20},{1,9},{5... | collective-permute-start | bytes 12296 | tf_op jit(solution)/shard_map/ppermute | solution.py:203
  4.8 0.7 %copy-start.1 = (f32[8,128]{1,0:T(8,128)S(1)}, f32[8,128]{1,0:T(8,128)}, u32[]{:S(2)}) copy-start(f32[8,128]{1,0:T(8,128)} %refs_0_.3) | copy-start | bytes 12292
  5.5 7.8 %copy-start.2 = (s32[1,64]{1,0:T(1,128)S(1)}, s32[1,64]{1,0:T(1,128)}, u32[]{:S(2)}) copy-start(s32[1,64]{1,0:T(1,128)} %rows.1) | copy-start | bytes 772
  5.5 7.8 %copy-start.3 = (s32[1,64]{1,0:T(1,128)S(1)}, s32[1,64]{1,0:T(1,128)}, u32[]{:S(2)}) copy-start(s32[1,64]{1,0:T(1,128)} %cols.1) | copy-start | bytes 772
  5.5 4.4 %collective-permute-start.1 = (f32[2,8,128]{2,1,0:T(8,128)S(1)}, f32[2,8,128]{2,1,0:T(8,128)S(1)}, u32[]{:S(2)}, u32[]{:S(2)}) collective-permute-start(f32[2,8,128]{2,1,0:T(8,128)S(1)} %shard_map.55.refs_0_), channel_id=1, source_target_pairs={{0,4},{4,0},{8,12},{12,8},{16,20},{20,16},{24,28},{28,24},{1,5},{5... | collective-permute-start | bytes 24584 | tf_op jit(solution)/shard_map/ppermute | solution.py:203
  7.5 1.2 %collective-permute-start.5 = (f32[8,128]{1,0:T(8,128)S(1)}, f32[8,128]{1,0:T(8,128)S(1)}, u32[]{:S(2)}, u32[]{:S(2)}) collective-permute-start(f32[8,128]{1,0:T(8,128)S(1)} %copy-done.1), channel_id=1, source_target_pairs={{0,1},{1,0},{2,3},{3,2},{4,5},{5,4},{6,7},{7,6},{8,9},{9,8},{10,11... | collective-permute-start | bytes 12296 | tf_op jit(solution)/shard_map/ppermute | solution.py:203
  8.7 5.9 %collective-permute-start.6 = (f32[2,8,128]{2,1,0:T(8,128)S(1)}, f32[2,8,128]{2,1,0:T(8,128)S(1)}, u32[]{:S(2)}, u32[]{:S(2)}) collective-permute-start(f32[2,8,128]{2,1,0:T(8,128)S(1)} %shard_map.59.refs_0_), channel_id=1, source_target_pairs={{0,3},{1,2},{2,1},{3,0},{4,7},{5,6},{6,5},{7,4},{8,11},{9,10},{10,... | collective-permute-start | bytes 24584 | tf_op jit(solution)/shard_map/ppermute | solution.py:203
  10.0 6.2 %collective-permute-start.2 = (f32[4,8,128]{2,1,0:T(8,128)S(1)}, f32[4,8,128]{2,1,0:T(8,128)S(1)}, u32[]{:S(2)}, u32[]{:S(2)}) collective-permute-start(f32[4,8,128]{2,1,0:T(8,128)S(1)} %shard_map.56.refs_0_), channel_id=1, source_target_pairs={{0,16},{4,20},{8,24},{12,28},{16,0},{20,4},{24,8},{28,12},{1,17},{... | collective-permute-start | bytes 49160 | tf_op jit(solution)/shard_map/ppermute | solution.py:203
  15.0 3.7 %collective-permute-start.7 = (f32[4,8,128]{2,1,0:T(8,128)S(1)}, f32[4,8,128]{2,1,0:T(8,128)S(1)}, u32[]{:S(2)}, u32[]{:S(2)}) collective-permute-start(f32[4,8,128]{2,1,0:T(8,128)S(1)} %get-tuple-element.24), channel_id=1, source_target_pairs={{0,4},{4,0},{8,12},{12,8},{16,20},{20,16},{24,28},{28,24},{1,5},{5... | collective-permute-start | bytes 49160 | tf_op jit(solution)/shard_map/ppermute | solution.py:203
  16.8 6.3 %collective-permute-start.3 = (f32[2,8,128]{2,1,0:T(8,128)S(1)}, f32[2,8,128]{2,1,0:T(8,128)S(1)}, u32[]{:S(2)}, u32[]{:S(2)}) collective-permute-start(f32[2,8,128]{2,1,0:T(8,128)S(1)} %get-tuple-element.20), channel_id=1, source_target_pairs={{0,3},{1,2},{2,1},{3,0},{4,7},{5,6},{6,5},{7,4},{8,11},{9,10},{10,... | collective-permute-start | bytes 24584 | tf_op jit(solution)/shard_map/ppermute | solution.py:203
  18.7 5.4 %collective-permute-start.10 = (f32[1,8,128]{2,1,0:T(8,128)S(1)}, f32[1,8,128]{2,1,0:T(8,128)S(1)}, u32[]{:S(2)}, u32[]{:S(2)}) collective-permute-start(f32[1,8,128]{2,1,0:T(8,128)S(1)} %get-tuple-element.28), channel_id=1, source_target_pairs={{0,24},{4,28},{8,16},{12,20},{16,8},{20,12},{24,0},{28,4},{1,25},{... | collective-permute-start | bytes 12296 | tf_op jit(solution)/shard_map/ppermute | solution.py:203
  20.1 4.5 %collective-permute-start.9 = (f32[1,8,128]{2,1,0:T(8,128)S(1)}, f32[1,8,128]{2,1,0:T(8,128)S(1)}, u32[]{:S(2)}, u32[]{:S(2)}) collective-permute-start(f32[1,8,128]{2,1,0:T(8,128)S(1)} %get-tuple-element.27), channel_id=1, source_target_pairs={{0,16},{4,20},{8,24},{12,28},{16,0},{20,4},{24,8},{28,12},{1,17},{... | collective-permute-start | bytes 12296 | tf_op jit(solution)/shard_map/ppermute | solution.py:203
  21.7 3.6 %collective-permute-start.8 = (f32[1,8,128]{2,1,0:T(8,128)S(1)}, f32[1,8,128]{2,1,0:T(8,128)S(1)}, u32[]{:S(2)}, u32[]{:S(2)}) collective-permute-start(f32[1,8,128]{2,1,0:T(8,128)S(1)} %get-tuple-element.26), channel_id=1, source_target_pairs={{0,8},{4,12},{8,0},{12,4},{16,24},{20,28},{24,16},{28,20},{1,9},{5... | collective-permute-start | bytes 12296 | tf_op jit(solution)/shard_map/ppermute | solution.py:203
  23.1 2.3 %collective-permute-start.4 = (f32[1,8,128]{2,1,0:T(8,128)S(1)}, f32[1,8,128]{2,1,0:T(8,128)S(1)}, u32[]{:S(2)}, u32[]{:S(2)}) collective-permute-start(f32[1,8,128]{2,1,0:T(8,128)S(1)} %get-tuple-element.22), channel_id=1, source_target_pairs={{0,1},{1,0},{2,3},{3,2},{4,5},{5,4},{6,7},{7,6},{8,9},{9,8},{10,11... | collective-permute-start | bytes 12296 | tf_op jit(solution)/shard_map/ppermute | solution.py:203

commit v4 on v3

--- a/solution.py
+++ b/solution.py
@@ -131,10 +131,6 @@
     return pltpu.roll(x, LANES // 2, 1)
 
 
-def wide(ref, q):
-    return jnp.concatenate([ref[q], ref[q + 1]], 1)
-
-
 def load(refs):
     out = []
     for ref in refs:
@@ -157,25 +153,30 @@
     xs, (hi, lo), outs = pieces(refs[:nx], take), refs[nx : nx + 2], places(refs[nx + 2 :], put)
     nv = xs[0].shape[0]
     left = jnp.concatenate([split(xs[k]) for k in range(len(xs))], 1).astype(bf16)
-    for q in range(0, len(outs), 2):
-        t = jnp.dot(left, wide(hi, q), preferred_element_type=f32) + jnp.dot(left, wide(lo, q), preferred_element_type=f32)
+    for pair in zip(put[::2], put[1::2]):
+        t = 0.0
+        for part in (hi, lo):
+            t += jnp.dot(left, jnp.concatenate([part[q] for q in pair], 1), preferred_element_type=f32)
         t = t[:nv] + t[nv:]
-        for i in range(2):
-            out, at = outs[q + i]
+        for i, q in enumerate(pair):
+            out, at = outs[q]
             out[at] = t[:, LANES * i : LANES * (i + 1)]
 
 
 def plain_kernel(nx, take, put, *refs):
     xs, (hi, lo), outs = pieces(refs[:nx], take), refs[nx : nx + 2], places(refs[nx + 2 :], put)
     nv = xs[0].shape[0]
+    first = min(put)
+    rows = slice(LANES * first, LANES * (max(put) + 1))
     total = 0.0
     for q in range(0, len(xs), 2):
         left = jnp.concatenate([split(xs[q]), split(xs[q + 1])], 1).astype(bf16)
         for part in (hi, lo):
-            total += lax.dot_general(left, wide(part, q), NT, preferred_element_type=f32)
+            right = jnp.concatenate([part[q, rows, :], part[q + 1, rows, :]], 1)
+            total += lax.dot_general(left, right, NT, preferred_element_type=f32)
     total = total[:nv] + total[nv:]
     for k, (out, at) in outs.items():
-        out[at] = total[:, LANES * k : LANES * (k + 1)]
+        out[at] = total[:, LANES * (k - first) : LANES * (k - first + 1)]
 
 
 def call(kernel, xs, hi, lo, outs, take, put):
@@ -190,12 +191,12 @@
     )(*xs, hi, lo)
 
 
-def turned_of(xs, hi, lo, outs, take, put):
-    return call(turned_kernel, xs, hi, lo, outs, take, put)
-
-
-def plain_of(xs, hi, lo, outs, take, put):
-    return call(plain_kernel, xs, hi, lo, outs, take, put)
+def turned_of(xs, hi, lo, take, put):
+    return call(turned_kernel, xs, hi, lo, (len(put),), take, put)[0]
+
+
+def plain_of(xs, hi, lo, take, put):
+    return call(plain_kernel, xs, hi, lo, (len(put),), take, put)[0]
 
 
 def trade(x, axis, step):
@@ -236,15 +237,17 @@
     n1 = trade(v, "col", 1)
     (c1,) = glue(join, [v, n1], 2)
     n2 = trade(c1, "col", 3)
-    t0, t1 = turned_of([c1, n2], hi, lo, (4, 4), (0, 1, 3, 2), (0, 2, 4, 6, 1, 3, 5, 7))
+    sent = turned_of([c1, n2], hi, lo, (0, 1, 3, 2), (1, 3, 5, 7))
+    kept = turned_of([c1, n2], hi, lo, (0, 1, 3, 2), (0, 2, 4, 6))
     x1 = trade(v, "row", 2)
     (s1,) = glue(join, [v, x1], 2)
     z1 = trade(s1, "row", 1)
     (s2,) = glue(join, [s1, z1], 4)
     z2 = trade(s2, "row", 4)
-    p0, p1 = plain_of([s2, z2], hi, lo, (2, 2), (0, 2, 1, 3, 4, 6, 5, 7), (0, 1, 3, 2))
-    u0, u2, u4, u6 = glue(add_parts, [t0, trade(t1, "row", 1)], 1, 1, 1, 1)
+    u0, u2, u4, u6 = glue(add_parts, [kept, trade(sent, "row", 1)], 1, 1, 1, 1)
     w = u0 + trade(u2, "row", 2) + trade(u4, "row", 4) + trade(u6, "row", 6)
+    p1 = plain_of([s2, z2], hi, lo, (0, 2, 1, 3, 4, 6, 5, 7), (3, 2))
+    p0 = plain_of([s2, z2], hi, lo, (0, 2, 1, 3, 4, 6, 5, 7), (0, 1))
     q0 = trade(p1, "col", 3)
     g0, g1 = glue(halve, [p0, q0], 1, 1)
     last = trade(g1, "col", 1)

time: 26.1 us -> 26 us (level)
  waiting for transfers between devices: 7.12 us -> 6.66 us
    ppermute x11, waiting for transfers between devices: 7.12 us -> 6.66 us  [trade(): return lax.ppermute(x, axis, [(i, i ^ step) for i in range(n)])]
    pallas_call x2 -> x4, Pallas kernels: 1.02 us -> 1.25 us  [call(): pl.pallas_call(functools.partial(kernel, len(xs), take, put), out_shape=[...]
  transfers between devices with their start and end apart: 11 -> 11, of which waited for: 6 -> 6; matrix products, arithmetic and copies ran while one was open for 0% -> 0% of each run, Pallas kernels for 9% -> 10%
where the time goes in v4:
time: 26 us; the launch traced here: 25.8 us
  starting transfers between devices  14.5 us (56%)
  waiting for transfers between devices  6.66 us (26%)
  Pallas kernels  2.6 us (10%)
  between operations  0.74 us (3%)
  local copies, waits for them, and re-layouts  0.7 us (3%)
  other arithmetic  0.6 us (2%)
    ppermute x11, starting transfers between devices, trade(): return lax.ppermute(x, axis, [(i, i ^ step) for i in range(n)])  14.5 us
    ppermute x11, waiting for transfers between devices, trade(): return lax.ppermute(x, axis, [(i, i ^ step) for i in range(n)])  6.66 us
    pallas_call x4, Pallas kernels, call(): pl.pallas_call(functools.partial(kernel, len(xs), take, put), out_shape=[...  1.25 us
    pallas_call x1, Pallas kernels, build(): pl.pallas_call(functools.partial(build_kernel, blk), out_shape=[jax.Shape...  1.18 us
    unnamed x8, local copies, waits for them, and re-layouts  0.7 us
    squeeze x1, other arithmetic, exchange(): return (g0 + last + w)[0]  0.6 us
  transfers between devices with their start and end apart: 11, of which 6 were waited for; matrix products, arithmetic and copies ran while one was open for 0% of the time, Pallas kernels for 10%

profile of v4, /device:TPU:0, one launch (start us, length us, event | category | flops | bytes accessed | tf_op | source)
XLA Modules:
  0.0 25.8 jit_solution(12030312074354173987)
XLA Ops:
  0.0 0.0 copy-start
  0.0 3.1 %collective-permute-start = (f32[8,128]{1,0:T(8,128)}, f32[8,128]{1,0:T(8,128)S(1)}, u32[]{:S(2)}, u32[]{:S(2)}) collective-permute-start(f32[8,128]{1,0:T(8,128)} %refs_0_.3), channel_id=1, source_target_pairs={{0,8},{4,12},{8,0},{12,4},{16,24},{20,28},{24,16},{28,20},{1,9},{5... | collective-permute-start | bytes 12296 | tf_op jit(solution)/shard_map/ppermute | solution.py:204
  3.1 1.8 %collective-permute-done.refs_1_ = f32[8,128]{1,0:T(8,128)S(1)} collective-permute-done((f32[8,128]{1,0:T(8,128)}, f32[8,128]{1,0:T(8,128)S(1)}, u32[]{:S(2)}, u32[]{:S(2)}) %collective-permute-start) | collective-permute-done | bytes 4128 | tf_op jit(solution)/shard_map/ppermute | solution.py:204
  4.8 0.0 copy-start.1
  4.9 0.7 %copy-done.1 = f32[8,128]{1,0:T(8,128)S(1)} copy-done((f32[8,128]{1,0:T(8,128)S(1)}, f32[8,128]{1,0:T(8,128)}, u32[]{:S(2)}) %copy-start.1) | copy-done | bytes 4120
  5.5 0.0 copy-start.2
  5.5 0.0 copy-start.3
  5.5 1.9 %collective-permute-start.1 = (f32[2,8,128]{2,1,0:T(8,128)S(1)}, f32[2,8,128]{2,1,0:T(8,128)S(1)}, u32[]{:S(2)}, u32[]{:S(2)}) collective-permute-start(f32[2,8,128]{2,1,0:T(8,128)S(1)} %shard_map.55.refs_0_), channel_id=1, source_target_pairs={{0,4},{4,0},{8,12},{12,8},{16,20},{20,16},{24,28},{28,24},{1,5},{5... | collective-permute-start | bytes 24584 | tf_op jit(solution)/shard_map/ppermute | solution.py:204
  7.5 0.0 collective-permute-start.5
  7.5 1.2 %collective-permute-done.5.refs_1_ = f32[8,128]{1,0:T(8,128)S(1)} collective-permute-done((f32[8,128]{1,0:T(8,128)S(1)}, f32[8,128]{1,0:T(8,128)S(1)}, u32[]{:S(2)}, u32[]{:S(2)}) %collective-permute-start.5) | collective-permute-done | bytes 4128 | tf_op jit(solution)/shard_map/ppermute | solution.py:204
  8.7 1.3 %collective-permute-start.6 = (f32[2,8,128]{2,1,0:T(8,128)S(1)}, f32[2,8,128]{2,1,0:T(8,128)S(1)}, u32[]{:S(2)}, u32[]{:S(2)}) collective-permute-start(f32[2,8,128]{2,1,0:T(8,128)S(1)} %shard_map.60.refs_0_), channel_id=1, source_target_pairs={{0,3},{1,2},{2,1},{3,0},{4,7},{5,6},{6,5},{7,4},{8,11},{9,10},{10,... | collective-permute-start | bytes 24584 | tf_op jit(solution)/shard_map/ppermute | solution.py:204
  9.9 0.0 collective-permute-done.1.refs_1_
  10.0 2.6 %collective-permute-start.2 = (f32[4,8,128]{2,1,0:T(8,128)S(1)}, f32[4,8,128]{2,1,0:T(8,128)S(1)}, u32[]{:S(2)}, u32[]{:S(2)}) collective-permute-start(f32[4,8,128]{2,1,0:T(8,128)S(1)} %shard_map.56.refs_0_), channel_id=1, source_target_pairs={{0,16},{4,20},{8,24},{12,28},{16,0},{20,4},{24,8},{28,12},{1,17},{... | collective-permute-start | bytes 49160 | tf_op jit(solution)/shard_map/ppermute | solution.py:204
  13.2 0.1 init.1.start
  13.3 0.0 copy-done
  13.4 0.0 copy-done.2
  13.4 0.0 copy-done.3
  13.4 1.2 %build.1 = (bf16[8,512,128]{2,1,0:T(8,128)(2,1)S(1)}, bf16[8,512,128]{2,1,0:T(8,128)(2,1)S(1)}, f32[8,512,128]{2,1,0:T(8,128)S(1)}) custom-call(f32[2048,128]{1,0:T(8,128)S(1)} %bitcast.7, s32[1,64]{1,0:T(1,128)S(1)} %copy-done.2, s32[1,64]{1,0:T(1,128)S(1)} %copy-done.3, s32[8,128]{1,0:T(8,128)S(1)} %count.2, ...), custom_call_target="tpu_custom_call", output_to_operand_aliasing={{2}: (4, {})} | custom-call | flops 1048576 | bytes 6291456 | tf_op jit(solution)/shard_map/build/pallas_call | solution.py:112
  14.6 0.0 collective-permute-done.6.refs_1_
  14.6 0.2 shard_map.62
  14.8 1.2 %collective-permute-start.7 = (f32[4,8,128]{2,1,0:T(8,128)S(1)}, f32[4,8,128]{2,1,0:T(8,128)S(1)}, u32[]{:S(2)}, u32[]{:S(2)}) collective-permute-start(f32[4,8,128]{2,1,0:T(8,128)S(1)} %shard_map.62), channel_id=1, source_target_pairs={{0,4},{4,0},{8,12},{12,8},{16,20},{20,16},{24,28},{28,24},{1,5},{5... | collective-permute-start | bytes 49160 | tf_op jit(solution)/shard_map/ppermute | solution.py:204
  16.0 0.0 collective-permute-done.2.refs_1_
  16.0 0.4 %shard_map.58 = f32[2,8,128]{2,1,0:T(8,128)S(1)} custom-call(f32[4,8,128]{2,1,0:T(8,128)S(1)} %shard_map.56.refs_0_, f32[4,8,128]{2,1,0:T(8,128)S(1)} %collective-permute-done.2.refs_1_, bf16[8,512,128]{2,1,0:T(8,128)(2,1)S(1)} %get-tuple-element.13.refs_2_, bf16[8,512,128]{2,1,0:T(8,128)(2,1)S(1)} %get-tuple-element.14.refs_3_), custom_call_target="tpu_custom_call" | custom-call | flops 67108864 | bytes 2097152 | tf_op jit(solution)/shard_map/pallas_call | solution.py:184
  16.4 0.0 collective-permute-start.3
  16.4 0.3 %shard_map.61.a = f32[4,8,128]{2,1,0:T(8,128)S(1)} custom-call(f32[2,8,128]{2,1,0:T(8,128)S(1)} %shard_map.60.refs_0_, f32[2,8,128]{2,1,0:T(8,128)S(1)} %collective-permute-done.6.refs_1_, bf16[8,512,128]{2,1,0:T(8,128)(2,1)S(1)} %get-tuple-element.13.refs_2_, bf16[8,512,128]{2,1,0:T(8,128)(2,1)S(1)} %get-tuple-element.14.refs_3_), custom_call_target="tpu_custom_call" | custom-call | flops 67108864 | bytes 2097152 | tf_op jit(solution)/shard_map/pallas_call | solution.py:184
  16.7 1.9 %collective-permute-done.7.b = f32[4,8,128]{2,1,0:T(8,128)S(1)} collective-permute-done((f32[4,8,128]{2,1,0:T(8,128)S(1)}, f32[4,8,128]{2,1,0:T(8,128)S(1)}, u32[]{:S(2)}, u32[]{:S(2)}) %collective-permute-start.7) | collective-permute-done | bytes 16416 | tf_op jit(solution)/shard_map/ppermute | solution.py:204
  18.6 1.3 %collective-permute-start.10 = (f32[1,8,128]{2,1,0:T(8,128)S(1)}, f32[1,8,128]{2,1,0:T(8,128)S(1)}, u32[]{:S(2)}, u32[]{:S(2)}) collective-permute-start(f32[1,8,128]{2,1,0:T(8,128)S(1)} %get-tuple-element.20), channel_id=1, source_target_pairs={{0,24},{4,28},{8,16},{12,20},{16,8},{20,12},{24,0},{28,4},{1,25},{... | collective-permute-start | bytes 12296 | tf_op jit(solution)/shard_map/ppermute | solution.py:204
  19.9 1.7 %collective-permute-start.9 = (f32[1,8,128]{2,1,0:T(8,128)S(1)}, f32[1,8,128]{2,1,0:T(8,128)S(1)}, u32[]{:S(2)}, u32[]{:S(2)}) collective-permute-start(f32[1,8,128]{2,1,0:T(8,128)S(1)} %get-tuple-element.19), channel_id=1, source_target_pairs={{0,16},{4,20},{8,24},{12,28},{16,0},{20,4},{24,8},{28,12},{1,17},{... | collective-permute-start | bytes 12296 | tf_op jit(solution)/shard_map/ppermute | solution.py:204
  21.6 1.3 %collective-permute-start.8 = (f32[1,8,128]{2,1,0:T(8,128)S(1)}, f32[1,8,128]{2,1,0:T(8,128)S(1)}, u32[]{:S(2)}, u32[]{:S(2)}) collective-permute-start(f32[1,8,128]{2,1,0:T(8,128)S(1)} %get-tuple-element.18), channel_id=1, source_target_pairs={{0,8},{4,12},{8,0},{12,4},{16,24},{20,28},{24,16},{28,20},{1,9},{5... | collective-permute-start | bytes 12296 | tf_op jit(solution)/shard_map/ppermute | solution.py:204
  23.0 0.4 %shard_map.57.a = f32[2,8,128]{2,1,0:T(8,128)S(1)} custom-call(f32[4,8,128]{2,1,0:T(8,128)S(1)} %shard_map.56.refs_0_, f32[4,8,128]{2,1,0:T(8,128)S(1)} %collective-permute-done.2.refs_1_, bf16[8,512,128]{2,1,0:T(8,128)(2,1)S(1)} %get-tuple-element.13.refs_2_, bf16[8,512,128]{2,1,0:T(8,128)(2,1)S(1)} %get-tuple-element.14.refs_3_), custom_call_target="tpu_custom_call" | custom-call | flops 67108864 | bytes 2097152 | tf_op jit(solution)/shard_map/pallas_call | solution.py:184
  23.3 0.0 collective-permute-done.3.b
  23.4 0.1 collective-permute-start.4
  23.4 0.5 %collective-permute-done.10 = f32[1,8,128]{2,1,0:T(8,128)S(1)} collective-permute-done((f32[1,8,128]{2,1,0:T(8,128)S(1)}, f32[1,8,128]{2,1,0:T(8,128)S(1)}, u32[]{:S(2)}, u32[]{:S(2)}) %collective-permute-start.10) | collective-permute-done | bytes 4128 | tf_op jit(solution)/shard_map/ppermute | solution.py:204
  24.0 0.4 %collective-permute-done.9 = f32[1,8,128]{2,1,0:T(8,128)S(1)} collective-permute-done((f32[1,8,128]{2,1,0:T(8,128)S(1)}, f32[1,8,128]{2,1,0:T(8,128)S(1)}, u32[]{:S(2)}, u32[]{:S(2)}) %collective-permute-start.9) | collective-permute-done | bytes 4128 | tf_op jit(solution)/shard_map/ppermute | solution.py:204
  24.4 0.8 %collective-permute-done.8 = f32[1,8,128]{2,1,0:T(8,128)S(1)} collective-permute-done((f32[1,8,128]{2,1,0:T(8,128)S(1)}, f32[1,8,128]{2,1,0:T(8,128)S(1)}, u32[]{:S(2)}, u32[]{:S(2)}) %collective-permute-start.8) | collective-permute-done | bytes 4128 | tf_op jit(solution)/shard_map/ppermute | solution.py:204
  25.2 0.0 collective-permute-done.4
  25.2 0.6 %add_bitcast_fusion = f32[8,128]{1,0:T(8,128)} fusion(f32[1,8,128]{2,1,0:T(8,128)S(1)} %collective-permute-done.10, f32[1,8,128]{2,1,0:T(8,128)S(1)} %collective-permute-done.9, f32[1,8,128]{2,1,0:T(8,128)S(1)} %get-tuple-element.17, f32[1,8,128]{2,1,0:T(8,128)S(1)} %collective-permute-done.8, f32[1,8,128]{2,1,0:T(8,128)S(1)} %get-tuple-element.15, ...), kind=kLoop, calls=%fused_computation | loop fusion | flops 5120 | bytes 28672 | tf_op jit(solution)/shard_map/squeeze | solution.py:254
  (6 shorter events, 0.0 us)
Async XLA Ops:
  0.0 13.3 %copy-start = (f32[64,4096]{1,0:T(8,128)S(1)}, f32[64,4096]{1,0:T(8,128)}, u32[]{:S(2)}) copy-start(f32[64,4096]{1,0:T(8,128)} %param.6) | copy-start | bytes 3145732
  0.0 4.8 %collective-permute-start = (f32[8,128]{1,0:T(8,128)}, f32[8,128]{1,0:T(8,128)S(1)}, u32[]{:S(2)}, u32[]{:S(2)}) collective-permute-start(f32[8,128]{1,0:T(8,128)} %refs_0_.3), channel_id=1, source_target_pairs={{0,8},{4,12},{8,0},{12,4},{16,24},{20,28},{24,16},{28,20},{1,9},{5... | collective-permute-start | bytes 12296 | tf_op jit(solution)/shard_map/ppermute | solution.py:204
  4.8 0.7 %copy-start.1 = (f32[8,128]{1,0:T(8,128)S(1)}, f32[8,128]{1,0:T(8,128)}, u32[]{:S(2)}) copy-start(f32[8,128]{1,0:T(8,128)} %refs_0_.3) | copy-start | bytes 12292
  5.5 7.8 %copy-start.2 = (s32[1,64]{1,0:T(1,128)S(1)}, s32[1,64]{1,0:T(1,128)}, u32[]{:S(2)}) copy-start(s32[1,64]{1,0:T(1,128)} %rows.1) | copy-start | bytes 772
  5.5 7.8 %copy-start.3 = (s32[1,64]{1,0:T(1,128)S(1)}, s32[1,64]{1,0:T(1,128)}, u32[]{:S(2)}) copy-start(s32[1,64]{1,0:T(1,128)} %cols.1) | copy-start | bytes 772
  5.5 4.4 %collective-permute-start.1 = (f32[2,8,128]{2,1,0:T(8,128)S(1)}, f32[2,8,128]{2,1,0:T(8,128)S(1)}, u32[]{:S(2)}, u32[]{:S(2)}) collective-permute-start(f32[2,8,128]{2,1,0:T(8,128)S(1)} %shard_map.55.refs_0_), channel_id=1, source_target_pairs={{0,4},{4,0},{8,12},{12,8},{16,20},{20,16},{24,28},{28,24},{1,5},{5... | collective-permute-start | bytes 24584 | tf_op jit(solution)/shard_map/ppermute | solution.py:204
  7.5 1.2 %collective-permute-start.5 = (f32[8,128]{1,0:T(8,128)S(1)}, f32[8,128]{1,0:T(8,128)S(1)}, u32[]{:S(2)}, u32[]{:S(2)}) collective-permute-start(f32[8,128]{1,0:T(8,128)S(1)} %copy-done.1), channel_id=1, source_target_pairs={{0,1},{1,0},{2,3},{3,2},{4,5},{5,4},{6,7},{7,6},{8,9},{9,8},{10,11... | collective-permute-start | bytes 12296 | tf_op jit(solution)/shard_map/ppermute | solution.py:204
  8.7 5.9 %collective-permute-start.6 = (f32[2,8,128]{2,1,0:T(8,128)S(1)}, f32[2,8,128]{2,1,0:T(8,128)S(1)}, u32[]{:S(2)}, u32[]{:S(2)}) collective-permute-start(f32[2,8,128]{2,1,0:T(8,128)S(1)} %shard_map.60.refs_0_), channel_id=1, source_target_pairs={{0,3},{1,2},{2,1},{3,0},{4,7},{5,6},{6,5},{7,4},{8,11},{9,10},{10,... | collective-permute-start | bytes 24584 | tf_op jit(solution)/shard_map/ppermute | solution.py:204
  10.0 6.1 %collective-permute-start.2 = (f32[4,8,128]{2,1,0:T(8,128)S(1)}, f32[4,8,128]{2,1,0:T(8,128)S(1)}, u32[]{:S(2)}, u32[]{:S(2)}) collective-permute-start(f32[4,8,128]{2,1,0:T(8,128)S(1)} %shard_map.56.refs_0_), channel_id=1, source_target_pairs={{0,16},{4,20},{8,24},{12,28},{16,0},{20,4},{24,8},{28,12},{1,17},{... | collective-permute-start | bytes 49160 | tf_op jit(solution)/shard_map/ppermute | solution.py:204
  14.8 3.7 %collective-permute-start.7 = (f32[4,8,128]{2,1,0:T(8,128)S(1)}, f32[4,8,128]{2,1,0:T(8,128)S(1)}, u32[]{:S(2)}, u32[]{:S(2)}) collective-permute-start(f32[4,8,128]{2,1,0:T(8,128)S(1)} %shard_map.62), channel_id=1, source_target_pairs={{0,4},{4,0},{8,12},{12,8},{16,20},{20,16},{24,28},{28,24},{1,5},{5... | collective-permute-start | bytes 49160 | tf_op jit(solution)/shard_map/ppermute | solution.py:204
  16.4 6.9 %collective-permute-start.3 = (f32[2,8,128]{2,1,0:T(8,128)S(1)}, f32[2,8,128]{2,1,0:T(8,128)S(1)}, u32[]{:S(2)}, u32[]{:S(2)}) collective-permute-start(f32[2,8,128]{2,1,0:T(8,128)S(1)} %shard_map.58), channel_id=1, source_target_pairs={{0,3},{1,2},{2,1},{3,0},{4,7},{5,6},{6,5},{7,4},{8,11},{9,10},{10,... | collective-permute-start | bytes 24584 | tf_op jit(solution)/shard_map/ppermute | solution.py:204
  18.6 5.4 %collective-permute-start.10 = (f32[1,8,128]{2,1,0:T(8,128)S(1)}, f32[1,8,128]{2,1,0:T(8,128)S(1)}, u32[]{:S(2)}, u32[]{:S(2)}) collective-permute-start(f32[1,8,128]{2,1,0:T(8,128)S(1)} %get-tuple-element.20), channel_id=1, source_target_pairs={{0,24},{4,28},{8,16},{12,20},{16,8},{20,12},{24,0},{28,4},{1,25},{... | collective-permute-start | bytes 12296 | tf_op jit(solution)/shard_map/ppermute | solution.py:204
  19.9 4.5 %collective-permute-start.9 = (f32[1,8,128]{2,1,0:T(8,128)S(1)}, f32[1,8,128]{2,1,0:T(8,128)S(1)}, u32[]{:S(2)}, u32[]{:S(2)}) collective-permute-start(f32[1,8,128]{2,1,0:T(8,128)S(1)} %get-tuple-element.19), channel_id=1, source_target_pairs={{0,16},{4,20},{8,24},{12,28},{16,0},{20,4},{24,8},{28,12},{1,17},{... | collective-permute-start | bytes 12296 | tf_op jit(solution)/shard_map/ppermute | solution.py:204
  21.6 3.6 %collective-permute-start.8 = (f32[1,8,128]{2,1,0:T(8,128)S(1)}, f32[1,8,128]{2,1,0:T(8,128)S(1)}, u32[]{:S(2)}, u32[]{:S(2)}) collective-permute-start(f32[1,8,128]{2,1,0:T(8,128)S(1)} %get-tuple-element.18), channel_id=1, source_target_pairs={{0,8},{4,12},{8,0},{12,4},{16,24},{20,28},{24,16},{28,20},{1,9},{5... | collective-permute-start | bytes 12296 | tf_op jit(solution)/shard_map/ppermute | solution.py:204
  23.4 1.9 %collective-permute-start.4 = (f32[1,8,128]{2,1,0:T(8,128)S(1)}, f32[1,8,128]{2,1,0:T(8,128)S(1)}, u32[]{:S(2)}, u32[]{:S(2)}) collective-permute-start(f32[1,8,128]{2,1,0:T(8,128)S(1)} %get-tuple-element.16), channel_id=1, source_target_pairs={{0,1},{1,0},{2,3},{3,2},{4,5},{5,4},{6,7},{7,6},{8,9},{9,8},{10,11... | collective-permute-start | bytes 12296 | tf_op jit(solution)/shard_map/ppermute | solution.py:204
